TPU v7x, 256 devices: a whole 4x4x8 slice. The times are simulated.
256 devices in a mesh: gx: 8 (over y, core), gy: 32 (over z, x).
Axes of the slice: x: 4, y: 4, z: 8, core: 2. Of those that a mesh axis runs over, the one named last changes fastest.
Arguments:
- state_mean: float32 [2, 512, 1024], P(None, 'gy', 'gx'), may hold values from -6 to 6
- state_spread: bfloat16 [2, 512, 1024, 128], P(None, 'gy', 'gx'), may hold values from -6 to 6
- obs_value: float32 [2, 8, 32, 4], replicated, may hold values from -8 to 8
- obs_var: float32 [2, 8, 32, 4], replicated, may hold values from 0.25 to 4
- obs_col: int32 [2, 8, 32, 4], replicated, may hold values from 0 to 127
- obs_row: int32 [2, 8, 32, 4], replicated, may hold values from 0 to 15
- obs_level: int32 [2, 8, 32, 4], replicated, may hold values from 0 to 1
Outputs:
- analysis_mean: float32 [2, 512, 1024], P(None, 'gy', 'gx')
- analysis_spread: bfloat16 [2, 512, 1024, 128], P(None, 'gy', 'gx')
All inputs are finite; a program needn't handle non-finite values.
Results may differ from a plain program's by a relative error of at most 0.011.
Values may be sent and summed in bfloat16 or wider, within the bound.
A program may use at most 64 MiB of HBM per device.

v0:
```python
import jax
import jax.numpy as jnp
from jax import lax
from jax.sharding import PartitionSpec as P

PRECISE = lax.Precision.HIGHEST


def taper(dist_sq, radius):
    ratio = jnp.sqrt(dist_sq) / radius
    ratio_safe = jnp.maximum(ratio, 1.0)
    inner_part = (((-0.25 * ratio + 0.5) * ratio + 0.625) * ratio - 5.0 / 3.0) * ratio * ratio + 1.0
    outer_part = (
        ((((ratio / 12.0 - 0.5) * ratio + 0.625) * ratio + 5.0 / 3.0) * ratio - 5.0) * ratio
        + 4.0
        - 2.0 / (3.0 * ratio_safe)
    )
    return jnp.where(ratio <= 1.0, inner_part, jnp.where(ratio < 2.0, outer_part, 0.0))


def add_panel(totals, panel, obs_x, obs_y, spread_rows, row_y, col_x, radius):
    panel_zb, panel_qb, panel_eb = panel
    members = spread_rows.shape[2]
    delta_x = (col_x[:, None] - obs_x[None, :]).astype(jnp.float32)
    delta_y = (row_y[:, None] - obs_y[None, :]).astype(jnp.float32)
    taper_vals = taper(delta_x * delta_x + delta_y * delta_y, radius)

    def per_level(operands):
        spread_lev, mean_inc, spread_inc = operands
        covariance = jnp.dot(spread_lev, panel_zb.T, preferred_element_type=jnp.float32) / (
            members - 1.0
        )
        gain_bf = (taper_vals * covariance).astype(jnp.bfloat16)
        mean_inc = mean_inc + jnp.dot(gain_bf, panel_eb, preferred_element_type=jnp.float32)
        spread_inc = spread_inc + jnp.dot(gain_bf, panel_qb, preferred_element_type=jnp.float32)
        return (mean_inc, spread_inc)

    return lax.map(per_level, (spread_rows, totals[0], totals[1]))


def body(state_mean, state_spread, obs_value, obs_var, obs_col, obs_row, obs_level):
    levels, rows_y, cols_x, members = state_spread.shape
    count_x = lax.axis_size("gx")
    count_y = lax.axis_size("gy")
    radius = count_x * cols_x // 2
    at_x = lax.axis_index("gx")
    at_y = lax.axis_index("gy")
    blocks = obs_value.shape[0]
    root_dof = jnp.sqrt(jnp.float32(members - 1))
    identity = jnp.eye(members, dtype=jnp.float32)
    cell_count = rows_y * cols_x
    cell_ids = jnp.arange(cell_count, dtype=jnp.int32)
    row_y = at_y * rows_y + cell_ids // cols_x
    col_x = at_x * cols_x + cell_ids % cols_x
    mean_now = state_mean.reshape(levels, cell_count)
    spread = state_spread.reshape(levels, cell_count, members)
    for block_idx in range(blocks):
        loc_x = obs_col[block_idx][at_x, at_y]
        loc_y = obs_row[block_idx][at_x, at_y]
        loc_lev = obs_level[block_idx][at_x, at_y]
        flat_cell = loc_y * cols_x + loc_x
        prior_obs = mean_now[loc_lev, flat_cell]
        panel_z = spread[loc_lev, flat_cell, :].astype(jnp.float32)
        obs_sd = jnp.sqrt(obs_var[block_idx][at_x, at_y])
        weighted = panel_z / (obs_sd[:, None] * root_dof)
        innov_norm = (obs_value[block_idx][at_x, at_y] - prior_obs) / obs_sd
        zeros_init = (
            jnp.zeros((levels, cell_count), jnp.float32),
            jnp.zeros((levels, cell_count, members), jnp.float32),
        )
        all_x = (
            jnp.arange(count_x, dtype=jnp.int32)[:, None, None] * cols_x + obs_col[block_idx]
        ).reshape(-1)
        all_y = (
            jnp.arange(count_y, dtype=jnp.int32)[None, :, None] * rows_y + obs_row[block_idx]
        ).reshape(-1)
        gram_term = jnp.dot(weighted.T, weighted, precision=PRECISE)
        proj_term = jnp.dot(weighted.T, innov_norm, precision=PRECISE)
        gram_all, proj_all = lax.psum((gram_term, proj_term), ("gx", "gy"))
        factor = jnp.linalg.cholesky(identity + gram_all)
        ens_weights = jax.scipy.linalg.cho_solve((factor, True), proj_all)
        panel_e = (innov_norm - jnp.dot(weighted, ens_weights, precision=PRECISE)) / obs_sd
        solved = jax.scipy.linalg.cho_solve((factor, True), weighted.T)
        panel_q = (root_dof / obs_sd)[:, None] * solved.T
        panel_zb = panel_z.astype(jnp.bfloat16)
        panel_qb = panel_q.astype(jnp.bfloat16)
        panel_eb = panel_e.astype(jnp.bfloat16)
        totals = add_panel(
            zeros_init,
            (
                lax.all_gather(panel_zb, ("gx", "gy"), axis=0, tiled=True),
                lax.all_gather(panel_qb, ("gx", "gy"), axis=0, tiled=True),
                lax.all_gather(panel_eb, ("gx", "gy"), axis=0, tiled=True),
            ),
            all_x,
            all_y,
            spread,
            row_y,
            col_x,
            radius,
        )
        mean_now = mean_now + totals[0]
        spread = (spread.astype(jnp.float32) - 0.5 * totals[1]).astype(jnp.bfloat16)
    return (
        mean_now.reshape(levels, rows_y, cols_x),
        spread.reshape(levels, rows_y, cols_x, members),
    )


def solution(mesh):
    return jax.shard_map(
        body,
        mesh=mesh,
        in_specs=(P(None, "gy", "gx"), P(None, "gy", "gx", None), P(), P(), P(), P(), P()),
        out_specs=(P(None, "gy", "gx"), P(None, "gy", "gx", None)),
        check_vma=False,
    )
```

profile of v0, /device:TPU:1, one launch (start us, length us, event | category | flops | bytes accessed | tf_op | source)
XLA Modules:
  0.0 903.8 jit_solution(16388274281650954638)
XLA Ops:
  10.6 1.4 gather_fusion
  15.4 66.7 %all-gather = bf16[256,4,128]{2,1,0:T(4,128)(2,1)S(1)} all-gather(bf16[1,4,128]{2,1,0:T(4,128)(2,1)S(1)} %bitcast.216), channel_id=1, replica_groups=mesh['gx'=8,'gy'=32] {'gx','gy'}, dimensions={0}, use_global_device_ids=true | all-gather | bytes 263168 | tf_op jit(solution)/shard_map/all_gather | solution.py:91
  86.8 75.3 %psum.29 = f32[128]{0:T(128)S(1)} all-reduce(f32[128]{0:T(128)S(1)} %convolution_bitcast_fusion.9), channel_id=1, replica_groups=mesh['gx'=8,'gy'=32] {'gx','gy'}, use_global_device_ids=true, to_apply=%region_3.5 | all-reduce | flops 128 | bytes 1024 | tf_op jit(solution)/shard_map/psum | solution.py:79
  162.1 98.1 %all-reduce.5.cloned.1.call-done = f32[128,128]{0,1:T(8,128)} async-done(((f32[128,128]{0,1:T(8,128)}), f32[128,128]{0,1:T(8,128)}) %all-reduce.5.cloned.1.call-update) | async-done | bytes 65552 | tf_op jit(solution)/shard_map/psum | solution.py:79
  262.0 11.7 %cholesky.44 = f32[128,128]{1,0:T(8,128)S(1)} custom-call(f32[128,128]{1,0:T(8,128)S(1)} %fusion.45), custom_call_target="Cholesky" | custom-call | tf_op jit(solution)/shard_map/jit(cholesky)/cholesky | solution.py:80
  275.1 9.8 %custom-call.22 = f32[1,128,128]{1,2,0:T(8,128)S(1)} custom-call(f32[1,128,128]{2,1,0:T(8,128)S(1)} %fusion.32), custom_call_target="InvertDiagBlocksLowerTriangular" | custom-call | tf_op jit(solution)/shard_map/jit(_cho_solve)/triangular_solve | solution.py:81
  285.3 59.9 %all-gather.1 = bf16[256,4,128]{2,1,0:T(4,128)(2,1)S(1)} all-gather(bf16[1,4,128]{2,1,0:T(4,128)(2,1)S(1)} %fusion.25), channel_id=1, replica_groups=mesh['gx'=8,'gy'=32] {'gx','gy'}, dimensions={0}, use_global_device_ids=true | all-gather | bytes 263168 | tf_op jit(solution)/shard_map/all_gather | solution.py:92
  346.0 76.5 %all-reduce = bf16[1024]{0:T(1024)(128)(2,1)S(1)} all-reduce(bf16[1024]{0:T(1024)(128)(2,1)S(1)} %dynamic-update-slice.2), channel_id=1, replica_groups=mesh['gx'=8,'gy'=32] {'gx','gy'}, use_global_device_ids=true, to_apply=%add | all-reduce | flops 1024 | bytes 4096
  422.7 34.6 %while.26 = (s32[]{:T(128)}, f32[2,2048]{1,0:T(2,128)S(1)}, f32[2,2048,128]{2,1,0:T(8,128)S(1)}, bf16[2,2048,128]{2,1,0:T(8,128)(2,1)}, bf16[1024,128]{1,0:T(8,1...) while((s32[]{:T(128)}, f32[2,2048]{1,0:T(2,128)S(1)}, ...), condition=%wide.region_5.9_spmd.clone, body=%wide.region_4.8_spmd.clone.sunk | while | flops 1157627904 | bytes 14736005 | solution.py:38
  422.7 14.7 %fusion.135 = bf16[2048,1024]{1,0:T(8,128)(2,1)S(1)} fusion(bf16[1024,128]{1,0:T(8,128)(2,1)S(1)} %get-tuple-element.386, s32[1024]{0:T(1024)S(1)} %get-tuple-element.391, s32[2048]{0:T(1024)S(1)} %get-tuple-element.392, s32[1024]{0:T(1024)S(1)} %get-tuple-element.389, s32[2048]{0:T(1024)S(1)} %get-tuple-element.390, ...), kind=kOutput, calls=%fused_computation.10.clone.1 | convolution fusion | flops 616562688 | bytes 5005824 | tf_op jit(solution)/shard_map/while/body/eval_jaxpr/dot_general | solution.py:30
  437.5 1.3 fusion.137
  440.0 14.7 %fusion.135 = bf16[2048,1024]{1,0:T(8,128)(2,1)S(1)} fusion(bf16[1024,128]{1,0:T(8,128)(2,1)S(1)} %get-tuple-element.386, s32[1024]{0:T(1024)S(1)} %get-tuple-element.391, s32[2048]{0:T(1024)S(1)} %get-tuple-element.392, s32[1024]{0:T(1024)S(1)} %get-tuple-element.389, s32[2048]{0:T(1024)S(1)} %get-tuple-element.390, ...), kind=kOutput, calls=%fused_computation.10.clone.1 | convolution fusion | flops 616562688 | bytes 5005824 | tf_op jit(solution)/shard_map/while/body/eval_jaxpr/dot_general | solution.py:30
  454.7 1.3 fusion.137
  457.4 1.5 subtract_convert_fusion.1
  461.2 62.8 %all-gather.2 = bf16[256,4,128]{2,1,0:T(4,128)(2,1)} all-gather(bf16[1,4,128]{2,1,0:T(4,128)(2,1)S(1)} %bitcast.217), channel_id=1, replica_groups=mesh['gx'=8,'gy'=32] {'gx','gy'}, dimensions={0}, use_global_device_ids=true | all-gather | bytes 263168 | tf_op jit(solution)/shard_map/all_gather | solution.py:91
  524.2 77.2 %psum.31 = f32[128]{0:T(128)S(1)} all-reduce(f32[128]{0:T(128)S(1)} %convolution_bitcast_fusion.5), channel_id=1, replica_groups=mesh['gx'=8,'gy'=32] {'gx','gy'}, use_global_device_ids=true, to_apply=%region_7.11 | all-reduce | flops 128 | bytes 1024 | tf_op jit(solution)/shard_map/psum | solution.py:79
  601.5 95.7 %all-reduce.7.cloned.1.call-done = f32[128,128]{0,1:T(8,128)} async-done(((f32[128,128]{0,1:T(8,128)}), f32[128,128]{0,1:T(8,128)}) %all-reduce.7.cloned.1.call-update) | async-done | bytes 65552 | tf_op jit(solution)/shard_map/psum | solution.py:79
  699.0 11.7 %cholesky.55 = f32[128,128]{1,0:T(8,128)S(1)} custom-call(f32[128,128]{1,0:T(8,128)S(1)} %fusion.39), custom_call_target="Cholesky" | custom-call | tf_op jit(solution)/shard_map/jit(cholesky)/cholesky | solution.py:80
  712.0 9.8 %custom-call.24 = f32[1,128,128]{1,2,0:T(8,128)S(1)} custom-call(f32[1,128,128]{2,1,0:T(8,128)S(1)} %fusion.33), custom_call_target="InvertDiagBlocksLowerTriangular" | custom-call | tf_op jit(solution)/shard_map/jit(_cho_solve)/triangular_solve | solution.py:81
  722.2 59.9 %all-gather.3 = bf16[256,4,128]{2,1,0:T(4,128)(2,1)S(1)} all-gather(bf16[1,4,128]{2,1,0:T(4,128)(2,1)S(1)} %fusion.24), channel_id=1, replica_groups=mesh['gx'=8,'gy'=32] {'gx','gy'}, dimensions={0}, use_global_device_ids=true | all-gather | bytes 263168 | tf_op jit(solution)/shard_map/all_gather | solution.py:92
  783.0 76.6 %all-reduce.1 = bf16[1024]{0:T(1024)(128)(2,1)S(1)} all-reduce(bf16[1024]{0:T(1024)(128)(2,1)S(1)} %dynamic-update-slice.3), channel_id=1, replica_groups=mesh['gx'=8,'gy'=32] {'gx','gy'}, use_global_device_ids=true, to_apply=%add.1 | all-reduce | flops 1024 | bytes 4096
  859.8 35.3 %while.27 = (s32[]{:T(128)}, f32[2,2048]{1,0:T(2,128)S(1)}, f32[2,2048,128]{2,1,0:T(8,128)S(1)}, bf16[2,2048,128]{2,1,0:T(8,128)(2,1)S(1)}, bf16[1024,128]{1,0:T...) while((s32[]{:T(128)}, f32[2,2048]{1,0:T(2,128)S(1)}, ...), condition=%wide.region_9.13_spmd.clone, body=%wide.region_8.12_spmd.clone.sunk | while | flops 1157627904 | bytes 14735497 | solution.py:38
  859.8 15.1 %fusion.144 = bf16[2048,1024]{1,0:T(8,128)(2,1)S(1)} fusion(bf16[1024,128]{1,0:T(8,128)(2,1)} %get-tuple-element.425, s32[1024]{0:T(1024)S(1)} %get-tuple-element.430, s32[2048]{0:T(1024)S(1)} %get-tuple-element.431, s32[1024]{0:T(1024)S(1)} %get-tuple-element.428, s32[2048]{0:T(1024)S(1)} %get-tuple-element.429, ...), kind=kOutput, calls=%fused_computation.24.clone.1 | convolution fusion | flops 616562688 | bytes 5005316 | tf_op jit(solution)/shard_map/while/body/eval_jaxpr/dot_general | solution.py:30
  877.5 15.1 %fusion.144 = bf16[2048,1024]{1,0:T(8,128)(2,1)S(1)} fusion(bf16[1024,128]{1,0:T(8,128)(2,1)} %get-tuple-element.425, s32[1024]{0:T(1024)S(1)} %get-tuple-element.430, s32[2048]{0:T(1024)S(1)} %get-tuple-element.431, s32[1024]{0:T(1024)S(1)} %get-tuple-element.428, s32[2048]{0:T(1024)S(1)} %get-tuple-element.429, ...), kind=kOutput, calls=%fused_computation.24.clone.1 | convolution fusion | flops 616562688 | bytes 5005316 | tf_op jit(solution)/shard_map/while/body/eval_jaxpr/dot_general | solution.py:30
  (112 shorter events, 32.5 us)
Async XLA Ops:
  7.2 253.0 %all-reduce.5.cloned.1.call-start = ((), (), s32[]{:S(2)}) async-start(), calls=%async_computation | async-start | bytes 131072 | tf_op jit(solution)/shard_map/psum | solution.py:79
  13.0 684.2 %all-reduce.7.cloned.1.call-start = ((), (), s32[]{:S(2)}) async-start(), calls=%async_computation.1 | async-start | bytes 131072 | tf_op jit(solution)/shard_map/psum | solution.py:79
  84.2 338.5 %copy-start.9 = (f32[4]{0:T(128)}, f32[4]{0:T(128)S(1)}, u32[]{:S(2)}) copy-start(f32[4]{0:T(128)S(1)} %get-tuple-element.152) | copy-start | bytes 52
  457.3 1.6 copy-start.3
  457.3 2.2 copy-start.7
  457.3 3.2 copy-start.2
  457.3 66.7 %copy-start.8 = (f32[4]{0:T(128)S(1)}, f32[4]{0:T(128)}, u32[]{:S(2)}) copy-start(f32[4]{0:T(128)} %fusion.62) | copy-start | bytes 52
  457.4 66.7 %copy-start.10 = (f32[4]{0:T(128)S(1)}, f32[4]{0:T(128)}, u32[]{:S(2)}) copy-start(f32[4]{0:T(128)} %copy-done.9) | copy-start | bytes 52
  457.4 264.7 %copy-start.6 = (f32[4]{0:T(128)S(1)}, f32[4]{0:T(128)}, u32[]{:S(2)}) copy-start(f32[4]{0:T(128)} %get-tuple-element.151) | copy-start | bytes 52
  457.4 402.4 %copy-start.4 = (s32[1024]{0:T(1024)S(1)}, s32[1024]{0:T(1024)}, u32[]{:S(2)}) copy-start(s32[1024]{0:T(1024)} %get-tuple-element.404) | copy-start | bytes 12292
  457.4 402.4 %copy-start.5 = (s32[1024]{0:T(1024)S(1)}, s32[1024]{0:T(1024)}, u32[]{:S(2)}) copy-start(s32[1024]{0:T(1024)} %get-tuple-element.402) | copy-start | bytes 12292
  460.6 399.2 %copy-start = (f32[2,2048]{1,0:T(2,128)}, f32[2,2048]{1,0:T(2,128)S(1)}, u32[]{:S(2)}) copy-start(f32[2,2048]{1,0:T(2,128)S(1)} %fusion.83) | copy-start | bytes 49156
  895.1 1.3 copy-start.1
Sparse Core Ops, SparseCore 0:
  14.1 246.0 all-reduce.4
  460.6 236.4 all-reduce.6
where the time goes:
time: 906 us; the launch traced here: 904 us
  blocking collectives  555 us (61%)
  waiting for transfers between devices  194 us (21%)
  matrix products  73.8 us (8%)
  other arithmetic  54.9 us (6%)
  between operations  14.4 us (2%)
  local copies, waits for them, and re-layouts  11.7 us (1%)
    psum x2, waiting for transfers between devices, body(): gram_all, proj_all = lax.psum((gram_term, proj_term), ('gx', 'gy'))  194 us
    unnamed x2, blocking collectives  153 us
    psum x2, blocking collectives, body(): gram_all, proj_all = lax.psum((gram_term, proj_term), ('gx', 'gy'))  153 us
    all_gather x2, blocking collectives, body(): lax.all_gather(panel_zb, ('gx', 'gy'), axis=0, tiled=True)  130 us
    all_gather x2, blocking collectives, body(): lax.all_gather(panel_qb, ('gx', 'gy'), axis=0, tiled=True)  120 us
    dot_general x4, matrix products, per_level(): jnp.dot(spread_lev, panel_zb.T, preferred_element_type=jnp.float32)  59.5 us
    another operation x6, other arithmetic, body(): factor = jnp.linalg.cholesky(identity + gram_all)  24.8 us
    another operation x4, other arithmetic, body(): ens_weights = jax.scipy.linalg.cho_solve((factor, True), proj_all)  20.9 us
  transfers between devices with their start and end apart: 2, of which 2 were waited for; matrix products, arithmetic and copies ran while one was open for 1% of the time, Pallas kernels for 0%

commit v1 on v0

v1 whole, which is shorter than its diff:
```python
import functools
import jax
import jax.numpy as jnp
from jax import lax
from jax.experimental import pallas as pl
from jax.experimental.pallas import tpu as pltpu
from jax.sharding import PartitionSpec as P

MESH = pl.DeviceIdType.MESH


def gather_kernel(nx, ny, cells_x, spread_hbm, mean_ref, idx_ref, z_ref, p_ref,
                  cells, send, rows, near, pnear, allz, allp,
                  load_sem, self_sem, send_sem, recv_sem, zsend, zrecv, psend, precv):
    ax = lax.axis_index("gx")
    ay = lax.axis_index("gy")
    load = pltpu.make_async_copy(spread_hbm, cells, load_sem)
    load.start()
    other = ax + 1 - 2 * lax.rem(ax, 2)
    barrier = pltpu.get_barrier_semaphore()

    def greet(o, carry):
        pl.semaphore_signal(barrier, inc=1, device_id=(ax, lax.rem(ay + o, ny)), device_id_type=MESH)
        return carry

    lax.fori_loop(1, ny, greet, 0)

    def greet_y(o, carry):
        pl.semaphore_signal(barrier, inc=1, device_id=(lax.rem(ax + o, nx), ay), device_id_type=MESH)
        return carry

    lax.fori_loop(1, nx, greet_y, 0)

    members = cells.shape[2]
    sub = lax.broadcasted_iota(jnp.int32, (16, members), 0)
    lane = lax.broadcasted_iota(jnp.int32, (1, members), 1)
    place = (lax.broadcasted_iota(jnp.int32, mean_ref.shape, 0) * cells_x
             + lax.broadcasted_iota(jnp.int32, mean_ref.shape, 1))
    load.wait()
    prior = []
    for b in range(2):
        prow = jnp.zeros((1, members), jnp.float32)
        for s in range(4):
            f = idx_ref[((b * nx + ax) * ny + ay) * 4 + s]
            tile = cells[f >> 4].astype(jnp.float32)
            row = jnp.sum(jnp.where(sub == (f & 15), tile, 0.0), axis=0, keepdims=True)
            rows[b * 4 + s:b * 4 + s + 1, :] = row
            val = jnp.where(place == f, mean_ref[...], 0.0)
            val = jnp.sum(jnp.sum(val, axis=0, keepdims=True), axis=1, keepdims=True)
            prow = prow + jnp.where(lane == 4 * ay + s, jnp.broadcast_to(val, (1, members)), 0.0)
        prior.append(prow)
    send[0] = rows[0:4, :].astype(jnp.bfloat16)
    send[1] = rows[4:8, :].astype(jnp.bfloat16)
    for b in range(2):
        hi = prior[b].astype(jnp.bfloat16).astype(jnp.float32)
        rows[2 * b:2 * b + 1, :] = hi
        rows[2 * b + 1:2 * b + 2, :] = prior[b] - hi
    send[2] = rows[0:4, :].astype(jnp.bfloat16)
    pl.semaphore_wait(barrier, ny - 1 + nx - 1)

    own = pltpu.make_async_copy(send, near.at[:, ay], self_sem.at[0])
    own.start()

    def spread_out(o, carry):
        to = lax.rem(ay + o, ny)
        pltpu.make_async_remote_copy(
            send, near.at[:, ay], send_sem.at[to], recv_sem.at[ay],
            device_id=(ax, to), device_id_type=MESH).start()
        return carry

    lax.fori_loop(1, ny, spread_out, 0)
    own.wait()

    def arrive(o, carry):
        frm = lax.rem(ay + o, ny)
        pltpu.make_async_remote_copy(
            send, near.at[:, frm], send_sem.at[frm], recv_sem.at[frm],
            device_id=(ax, frm), device_id_type=MESH).wait()
        return carry

    lax.fori_loop(1, ny, arrive, 0)

    keep = pltpu.make_async_copy(near.at[0:2], allz.at[ax], self_sem.at[1])
    keep.start()

    def zcopy(src, slot, to):
        return pltpu.make_async_remote_copy(src, allz.at[slot], zsend.at[slot], zrecv.at[slot],
                                            device_id=(to, ay), device_id_type=MESH)

    def zout(o, carry):
        to = lax.rem(ax + 2 * o, nx)
        pltpu.make_async_remote_copy(near.at[0:2], allz.at[ax], zsend.at[to], zrecv.at[ax],
                                     device_id=(to, ay), device_id_type=MESH).start()
        return carry

    lax.fori_loop(1, nx // 2, zout, 0)
    pltpu.make_async_remote_copy(near.at[0:2], allz.at[ax], zsend.at[other], zrecv.at[ax],
                                 device_id=(other, ay), device_id_type=MESH).start()
    ptile = near[2].astype(jnp.float32)
    psum = jnp.sum(ptile, axis=0)
    pnear[0:1, :] = psum[0:1, :] + psum[1:2, :]
    pnear[1:2, :] = psum[2:3, :] + psum[3:4, :]
    allp[ax] = pnear[...]

    def pout(o, carry):
        to = lax.rem(ax + o, nx)
        pltpu.make_async_remote_copy(pnear, allp.at[ax], psend.at[to], precv.at[ax],
                                     device_id=(to, ay), device_id_type=MESH).start()
        return carry

    lax.fori_loop(1, nx, pout, 0)

    def relay(o, carry):
        g = lax.rem(ax + 2 * o, nx)
        pltpu.make_async_remote_copy(near.at[0:2], allz.at[g], zsend.at[g], zrecv.at[g],
                                     device_id=(g, ay), device_id_type=MESH).wait()
        pltpu.make_async_remote_copy(allz.at[g], allz.at[g], zsend.at[lax.rem(g + 1 - 2 * lax.rem(g, 2) + nx, nx)],
                                     zrecv.at[g], device_id=(other, ay), device_id_type=MESH).start()
        return carry

    lax.fori_loop(1, nx // 2, relay, 0)

    def settle(o, carry):
        g = lax.rem(ax + 2 * o, nx)
        h = g + 1 - 2 * lax.rem(g, 2)
        pltpu.make_async_remote_copy(allz.at[h], allz.at[h], zsend.at[h], zrecv.at[h],
                                     device_id=(other, ay), device_id_type=MESH).wait()
        return carry

    lax.fori_loop(0, nx // 2, settle, 0)

    def settle_p(o, carry):
        g = lax.rem(ax + o, nx)
        pltpu.make_async_remote_copy(pnear, allp.at[g], psend.at[g], precv.at[g],
                                     device_id=(g, ay), device_id_type=MESH).wait()
        return carry

    lax.fori_loop(1, nx, settle_p, 0)
    keep.wait()
    p_ref[...] = allp[...]
    outs = [pltpu.make_async_copy(allz.at[:, b], z_ref.at[b], self_sem.at[b]) for b in range(2)]
    for c in outs:
        c.start()
    for c in outs:
        c.wait()


def gather(nx, ny, spread, mean, idx):
    members = spread.shape[2]
    cells_x = mean.shape[1]
    bf, f32 = jnp.bfloat16, jnp.float32
    vm = pl.BlockSpec(memory_space=pltpu.VMEM)
    dma = pltpu.SemaphoreType.DMA
    return pl.pallas_call(
        functools.partial(gather_kernel, nx, ny, cells_x),
        out_shape=(jax.ShapeDtypeStruct((2, nx, ny, 4, members), bf), jax.ShapeDtypeStruct((nx, 8, members), f32)),
        in_specs=[pl.BlockSpec(memory_space=pl.ANY), vm, pl.BlockSpec(memory_space=pltpu.SMEM)],
        out_specs=(pl.BlockSpec(memory_space=pl.ANY), vm),
        scratch_shapes=[
            pltpu.VMEM(spread.shape, bf),
            pltpu.VMEM((3, 4, members), bf),
            pltpu.VMEM((8, members), f32),
            pltpu.VMEM((3, ny, 4, members), bf),
            pltpu.VMEM((8, members), f32),
            pltpu.VMEM((nx, 2, ny, 4, members), bf),
            pltpu.VMEM((nx, 8, members), f32),
            dma, dma((2,)), dma((ny,)), dma((ny,)), dma((nx,)), dma((nx,)), dma((nx,)), dma((nx,)),
        ],
        compiler_params=pltpu.CompilerParams(collective_id=0, has_side_effects=True, vmem_limit_bytes=60 << 20),
    )(spread, mean, idx)


HI = lax.Precision.HIGHEST
BF = jnp.bfloat16
F32 = jnp.float32


def mm(a, b):
    return jnp.dot(a, b, preferred_element_type=F32)


def split3(x):
    a = x.astype(BF)
    r = x - a.astype(F32)
    b = r.astype(BF)
    return a, b, (r - b.astype(F32)).astype(BF)


def taper_scaled(t, scale):
    rs = lax.rsqrt(t)
    r = t * rs
    c = scale
    inner = (((-0.25 * c * r + 0.5 * c) * r + 0.625 * c) * r - 5.0 / 3.0 * c) * t + c
    m = jnp.maximum(2.0 - r, 0.0)
    m = m * m
    m = m * m
    outer = m * ((r * (c / 12.0) + c / 6.0) - rs * (c / 24.0))
    return jnp.where(t <= 1.0, inner, outer)


def columns(row, out):
    for i in range(row.shape[1] // 128):
        tile = jnp.broadcast_to(row[:, i * 128:(i + 1) * 128], (128, 128))
        out[i * 128:(i + 1) * 128, :] = tile.T


def chain(zx, zt, qx, dcol, ivcol, z_f32, ivar_row):
    count, members = z_f32.shape
    dof = members - 1.0
    lane = lax.broadcasted_iota(jnp.int32, (count, members), 1)
    d1, d2, d3 = split3(dcol[...])
    zero = jnp.zeros((), BF)
    zx[:, :members] = z_f32.astype(BF)
    zx[:, members:] = jnp.where(lane == 0, d1.astype(F32), jnp.where(
        lane == 1, d2.astype(F32), jnp.where(lane == 2, d3.astype(F32), 0.0))).astype(BF)
    z_t = z_f32.T
    zt[...] = z_t.astype(BF)
    h1, h2, h3 = split3(z_t * (ivar_row * (1.0 / dof)))
    rhs = zx[...]
    full = mm(h1, rhs) + mm(h2, rhs) + mm(h3, rhs)
    row_i = lax.broadcasted_iota(jnp.int32, (members, members), 0)
    col_i = lax.broadcasted_iota(jnp.int32, (members, members), 1)
    eye = jnp.where(row_i == col_i, 1.0, 0.0).astype(F32)
    gram = full[:, :members] + eye
    vec = jnp.broadcast_to(jnp.sum(full[:, members:], axis=1, keepdims=True), (members, members))
    top = jnp.max(jnp.sum(jnp.abs(gram), axis=1, keepdims=True))
    scale = 2.0 / (1.0 + top)
    first = scale * (2.0 * eye - scale * gram)

    def more(state):
        step, miss, _ = state
        return jnp.logical_and(step < 60, miss > 1e-3)

    def newton(state):
        step, _, x = state
        resid = eye - jnp.dot(gram, x, precision=HI, preferred_element_type=F32)
        x = x + jnp.dot(x, resid, precision=HI, preferred_element_type=F32)
        return step + 1, jnp.max(jnp.abs(resid)), x

    _, _, inv = lax.while_loop(more, newton, (jnp.int32(0), jnp.float32(1.0), first))
    w = jnp.dot(inv, vec, precision=HI, preferred_element_type=F32)
    r1, r2, r3 = split3(jnp.concatenate([inv, -w], axis=1))
    row_e = lax.broadcasted_iota(jnp.int32, (members, 2 * members), 0)
    col_e = lax.broadcasted_iota(jnp.int32, (members, 2 * members), 1)
    ones = jnp.where(jnp.logical_and(row_e < 3, col_e >= members), 1.0, 0.0).astype(BF)
    z_b = rhs[:, :members]
    acc = mm(rhs, jnp.concatenate([r1, ones], axis=0)) + mm(z_b, r2) + mm(z_b, r3)
    iv = ivcol[...]
    qx[...] = (acc * jnp.concatenate([iv, iv], axis=1)).astype(BF)


def update_kernel(nx, ny, radius, spread_ref, mean_ref, z_ref, p_ref, meta_ref, mean_out, spread_out,
                  zx, zt, qx, z1, dcol, ivcol, xcol, ycol, dx2, macc):
    ax = lax.axis_index("gx")
    ay = lax.axis_index("gy")
    levels, rows_y, cols_x, members = spread_ref.shape
    count = z1.shape[0]
    inv_sq = 1.0 / (radius * radius)
    unit = 1.0 / (members - 1.0)
    prior = [jnp.concatenate([p_ref[i, b:b + 1, :] for i in range(nx)], axis=1) for b in range(2)]
    meta = [[meta_ref[4 * b + c:4 * b + c + 1, :] for c in range(4)] for b in range(2)]
    columns(meta[0][3] - prior[0], dcol)
    columns(1.0 / meta[0][2], ivcol)
    chain(zx, zt.at[0], qx.at[0], dcol, ivcol, z_ref[0].astype(F32).reshape(count, members), 1.0 / meta[0][2])
    columns(meta[1][3] - prior[1], dcol)
    columns(1.0 / meta[1][2], ivcol)
    columns(meta[1][0], xcol)
    columns(meta[1][1], ycol)
    z1[...] = z_ref[1].astype(F32).reshape(count, members).astype(BF)

    def cross(c, carry):
        rows = pl.ds(pl.multiple_of(c * 128, 128), 128)
        x_c, y_c = xcol[rows, :], ycol[rows, :]
        parts = []
        z_c = z1[rows, :]
        for i in range(count // 128):
            cut = slice(i * 128, (i + 1) * 128)
            ddx = x_c - meta[0][0][:, cut]
            ddy = y_c - meta[0][1][:, cut]
            t = (ddx * ddx + ddy * ddy) * inv_sq + 1e-30
            cov = mm(z_c, zt[0, :, cut])
            parts.append((taper_scaled(t, unit) * cov).astype(BF))
        inc = mm(jnp.concatenate(parts, axis=1), qx[0])
        z1[rows, :] = (z_c.astype(F32) - 0.5 * inc[:, :members]).astype(BF)
        dcol[rows, :] = dcol[rows, :] - inc[:, members:]
        return carry

    lax.fori_loop(0, count // 128, cross, 0)
    chain(zx, zt.at[1], qx.at[1], dcol, ivcol, z1[...].astype(F32), 1.0 / meta[1][2])

    col_x = (ax * cols_x + lax.broadcasted_iota(jnp.int32, (cols_x, 1), 0)).astype(F32)
    for b in range(2):
        ddx = col_x - meta[b][0]
        dx2[b] = ddx * ddx * inv_sq + 1e-30
    macc[...] = jnp.zeros_like(macc)
    lane = lax.broadcasted_iota(jnp.int32, (cols_x, members), 1)

    def sweep(y, carry):
        here = (ay * rows_y + y).astype(F32)
        s = [spread_ref[lev, y] for lev in range(levels)]
        for b in range(2):
            ddy = here - meta[b][1]
            dy2 = ddy * ddy * inv_sq
            parts = [[] for _ in range(levels)]
            for i in range(count // 128):
                cut = slice(i * 128, (i + 1) * 128)
                tap = taper_scaled(dx2[b, :, cut] + dy2[:, cut], unit)
                for lev in range(levels):
                    cov = mm(s[lev], zt[b, :, cut])
                    parts[lev].append((tap * cov).astype(BF))
            for lev in range(levels):
                inc = mm(jnp.concatenate(parts[lev], axis=1), qx[b])
                s[lev] = (s[lev].astype(F32) - 0.5 * inc[:, :members]).astype(BF)
                macc[...] += jnp.where(lane == lev * rows_y + y, inc[:, members:], 0.0)
        for lev in range(levels):
            spread_out[lev, y] = s[lev]
        return carry

    lax.fori_loop(0, rows_y, sweep, 0)
    mean_out[...] = mean_ref[...] + macc[...].T[:levels * rows_y, :]


def update(nx, ny, radius, spread, mean, z, p, meta):
    levels, rows_y, cols_x, members = spread.shape
    count = meta.shape[1]
    vm = pl.BlockSpec(memory_space=pltpu.VMEM)
    return pl.pallas_call(
        functools.partial(update_kernel, nx, ny, radius),
        out_shape=(jax.ShapeDtypeStruct(mean.shape, F32), jax.ShapeDtypeStruct(spread.shape, BF)),
        in_specs=[vm] * 5,
        out_specs=(vm, vm),
        scratch_shapes=[
            pltpu.VMEM((count, 2 * members), BF),
            pltpu.VMEM((2, members, count), BF),
            pltpu.VMEM((2, count, 2 * members), BF),
            pltpu.VMEM((count, members), BF),
            pltpu.VMEM((count, members), F32),
            pltpu.VMEM((count, members), F32),
            pltpu.VMEM((count, members), F32),
            pltpu.VMEM((count, members), F32),
            pltpu.VMEM((2, cols_x, count), F32),
            pltpu.VMEM((cols_x, members), F32),
        ],
        compiler_params=pltpu.CompilerParams(vmem_limit_bytes=60 << 20),
    )(spread, mean, z, p, meta)


def body(state_mean, state_spread, obs_value, obs_var, obs_col, obs_row, obs_level):
    levels, rows_y, cols_x, members = state_spread.shape
    nx, ny = lax.axis_size("gx"), lax.axis_size("gy")
    radius = nx * cols_x // 2
    spread = state_spread.reshape(levels * rows_y * cols_x // 16, 16, members)
    mean = state_mean.reshape(levels * rows_y, cols_x)
    idx = ((obs_level * rows_y + obs_row) * cols_x + obs_col).reshape(-1)
    z, p = gather(nx, ny, spread, mean, idx)
    obs_x = (jnp.arange(nx, dtype=jnp.int32)[None, :, None, None] * cols_x + obs_col).astype(F32)
    obs_y = (jnp.arange(ny, dtype=jnp.int32)[None, None, :, None] * rows_y + obs_row).astype(F32)
    meta = jnp.stack([obs_x, obs_y, obs_var, obs_value], axis=1).reshape(8, -1)
    new_mean, new_spread = update(nx, ny, radius, state_spread, mean, z, p, meta)
    return new_mean.reshape(state_mean.shape), new_spread


def solution(mesh):
    return jax.shard_map(
        body,
        mesh=mesh,
        in_specs=(P(None, "gy", "gx"), P(None, "gy", "gx", None), P(), P(), P(), P(), P()),
        out_specs=(P(None, "gy", "gx"), P(None, "gy", "gx", None)),
        check_vma=False,
    )
```

time: 906 us -> 71.4 us (0.08)
  blocking collectives: 555 us -> 0 us
  waiting for transfers between devices: 194 us -> 0 us
  matrix products: 73.8 us -> 0 us
  Pallas kernels: 0 us -> 67 us
  other arithmetic: 54.9 us -> 0.92 us
  between operations: 14.4 us -> 0.69 us
    all_gather x4 -> x0, blocking collectives: 249 us -> none  [the longest x2 130 us: body(): lax.all_gather(panel_zb, ('gx', 'gy'), axis=0, tiled=True)]
    psum x2 -> x0, waiting for transfers between devices: 194 us -> none  [body(): gram_all, proj_all = lax.psum((gram_term, proj_term), ('gx', 'gy'))]
    unnamed x2 -> x0, blocking collectives: 153 us -> none
    psum x2 -> x0, blocking collectives: 153 us -> none  [body(): gram_all, proj_all = lax.psum((gram_term, proj_term), ('gx', 'gy'))]
    dot_general x18 -> x0, matrix products: 72.3 us -> none  [the longest x4 59.5 us: per_level(): jnp.dot(spread_lev, panel_zb.T, preferred_element_type=jnp.float32)]
    pallas_call x0 -> x2, Pallas kernels: none -> 67 us  [the longest x1 40.6 us: update(): pl.pallas_call(functools.partial(update_kernel, nx, ny, radius), out_shap...]
    another operation x10 -> x2, other arithmetic: 45.7 us -> 0.92 us  [body(): meta = jnp.stack([obs_x, obs_y, obs_var, obs_value], axis=1).reshape(8, -1)]
  transfers between devices with their start and end apart: 2 -> 0, of which waited for: 2 -> 0; matrix products, arithmetic and copies ran while one was open for 1% -> 0% of each run, Pallas kernels for 0% -> 0%
where the time goes in v1:
time: 71.4 us; the launch traced here: 71.3 us
  Pallas kernels  67 us (94%)
  local copies, waits for them, and re-layouts  2.68 us (4%)
  other arithmetic  0.92 us (1%)
    pallas_call x1, Pallas kernels, update(): pl.pallas_call(functools.partial(update_kernel, nx, ny, radius), out_shap...  40.6 us
    pallas_call x1, Pallas kernels, gather(): pl.pallas_call(functools.partial(gather_kernel, nx, ny, cells_x), out_sha...  26.4 us

profile of v1, /device:TPU:1, one launch (start us, length us, event | category | flops | bytes accessed | tf_op | source)
XLA Modules:
  0.0 71.3 jit_solution(3599019234795380922)
XLA Ops:
  0.6 0.0 copy-start
  0.7 0.0 copy-start.1
  0.7 0.9 %convert_bitcast_fusion.1 = (f32[2,1,8,32,4]{3,4,2,0,1:T(4,128)S(1)}, s32[2,8,32,4]{2,3,1,0:T(4,128)S(1)}, f32[2,1,8,32,4]{3,4,2,0,1:T(4,128)S(1)}) fusion(s32[2,8,32,4]{2,3,1,0:T(4,128)} %param.11, s32[8]{0:T(128)S(1)} %iota_multiply_fusion.1, s32[2,8,32,4]{2,3,1,0:T(4,128)} %param.12, s32[2,8,32,4]{2,3,1,0:T(4,128)} %param.13, s32[32]{0:T(128)S(1)} %iota_multiply_fusion), kind=kLoop, calls=%fused_computation.2 | loop fusion | flops 16384 | bytes 49312 | tf_op jit(solution)/shard_map/stack | solution.py:358
  1.6 0.0 copy-done
  1.6 0.0 copy-done.1
  1.6 0.5 copy.11
  2.1 1.3 %reshape.32.meta_ref = f32[8,1024]{1,0:T(8,128)} reshape(f32[2,4,8,32,4]{4,3,2,1,0:T(8,128)S(1)} %copy.11) | data formatting | bytes 65536 | tf_op jit(solution)/shard_map/reshape | solution.py:358
  3.3 0.2 copy.10
  3.5 0.8 %reshape.31.idx_ref = s32[2048]{0:T(1024)} reshape(s32[2,8,32,4]{3,2,1,0:T(8,128)S(1)} %copy.10) | data formatting | bytes 16384 | tf_op jit(solution)/shard_map/reshape | solution.py:354
  4.3 26.4 %shard_map.86 = (bf16[2,8,32,4,128]{4,3,2,1,0:T(4,128)(2,1)}, f32[8,8,128]{2,1,0:T(8,128)}) custom-call(bf16[256,16,128]{2,1,0:T(8,128)(2,1)} %bitcast.13, f32[32,128]{1,0:T(8,128)} %bitcast.14, s32[2048]{0:T(1024)} %reshape.31.idx_ref), custom_call_target="tpu_custom_call" | custom-call | tf_op jit(solution)/shard_map/pallas_call | solution.py:154
  30.7 40.6 %shard_map.87 = (f32[32,128]{1,0:T(8,128)}, bf16[2,16,128,128]{3,2,1,0:T(8,128)(2,1)}) custom-call(bf16[2,16,128,128]{3,2,1,0:T(8,128)(2,1)} %spread_ref.1, f32[32,128]{1,0:T(8,128)} %bitcast.15, bf16[2,8,32,4,128]{4,3,2,1,0:T(4,128)(2,1)} %get-tuple-element.6.z_ref, f32[8,8,128]{2,1,0:T(8,128)} %get-tuple-element.7.p_ref, f32[8,1024]{1,0:T(8,128)} %reshape.32.meta_ref), custom_call_target="tpu_custom_call" | custom-call | tf_op jit(solution)/shard_map/pallas_call | solution.py:327
  (3 shorter events, 0.0 us)
Async XLA Ops:
  0.6 0.9 %copy-start = (f32[2,8,32,4]{2,3,1,0:T(4,128)S(1)}, f32[2,8,32,4]{2,3,1,0:T(4,128)}, u32[]{:S(2)}) copy-start(f32[2,8,32,4]{2,3,1,0:T(4,128)} %param.9) | copy-start | bytes 24580
  0.7 0.9 %copy-start.1 = (f32[2,8,32,4]{2,3,1,0:T(4,128)S(1)}, f32[2,8,32,4]{2,3,1,0:T(4,128)}, u32[]{:S(2)}) copy-start(f32[2,8,32,4]{2,3,1,0:T(4,128)} %param.10) | copy-start | bytes 24580

commit v2 on v1

v2 whole, which is shorter than its diff:
```python
import functools
import jax
import jax.numpy as jnp
from jax import lax
from jax.experimental import pallas as pl
from jax.experimental.pallas import tpu as pltpu
from jax.sharding import PartitionSpec as P

MESH = pl.DeviceIdType.MESH
HI = lax.Precision.HIGHEST
BF = jnp.bfloat16
F32 = jnp.float32
PER = 4
SPLIT = (4, 20, 12)


def mm(a, b):
    return jnp.dot(a, b, preferred_element_type=F32)


def exact(a, b):
    return jnp.dot(a, b, precision=HI, preferred_element_type=F32)


def split3(x):
    a = x.astype(BF)
    r = x - a.astype(F32)
    b = r.astype(BF)
    return a, b, (r - b.astype(F32)).astype(BF)


def taper_scaled(t, c):
    rs = lax.rsqrt(t)
    r = t * rs
    inner = (((-0.25 * c * r + 0.5 * c) * r + 0.625 * c) * r - 5.0 / 3.0 * c) * t + c
    m = jnp.maximum(2.0 - r, 0.0)
    m = m * m
    m = m * m
    outer = m * ((r * (c / 12.0) + c / 6.0) - rs * (c / 24.0))
    return jnp.where(t <= 1.0, inner, outer)


def columns(rows8, out):
    turned = jnp.broadcast_to(rows8[:, None, :], (8, 16, 128)).reshape(128, 128).T
    for i in range(8):
        out[i * 128:(i + 1) * 128, :] = jnp.broadcast_to(turned[:, 16 * i:16 * i + 1], (128, 128))


def wide(rows8):
    return jnp.concatenate([rows8[i:i + 1, :] for i in range(8)], axis=1)


def gather_kernel(nx, ny, radius, cols_x, rows_y, spread_hbm, mean_ref, col_ref, row_ref, lev_ref, var_ref, val_ref,
                  z_ref, p_ref, meta_ref, tap_ref,
                  cells, send, rows, near, pnear, allz, allp, dx2, xcol, ycol, tap,
                  load_sem, self_sem, tap_sem, send_sem, recv_sem, zsend, zrecv, psend, precv):
    ax = lax.axis_index("gx")
    ay = lax.axis_index("gy")
    load = pltpu.make_async_copy(spread_hbm, cells, load_sem)
    load.start()
    other = ax + 1 - 2 * lax.rem(ax, 2)
    barrier = pltpu.get_barrier_semaphore()

    def greet(o, carry):
        pl.semaphore_signal(barrier, inc=1, device_id=(ax, lax.rem(ay + o, ny)), device_id_type=MESH)
        return carry

    lax.fori_loop(1, ny, greet, 0)

    def greet_x(o, carry):
        pl.semaphore_signal(barrier, inc=1, device_id=(lax.rem(ax + o, nx), ay), device_id_type=MESH)
        return carry

    lax.fori_loop(1, nx, greet_x, 0)

    members = cells.shape[1]
    total = cells.shape[0]
    lane = lax.broadcasted_iota(jnp.int32, (1, members), 1)
    place = (lax.broadcasted_iota(jnp.int32, mean_ref.shape, 0) * cols_x
             + lax.broadcasted_iota(jnp.int32, mean_ref.shape, 1)).astype(F32)

    mine = []
    for b in range(2):
        at = b * nx + ax
        flat = (lev_ref[at] * rows_y + row_ref[at]) * cols_x + col_ref[at]
        pick = lax.broadcasted_iota(jnp.int32, flat.shape, 1) == ay
        mine.append(jnp.sum(jnp.where(pick, flat.astype(F32), 0.0), axis=1, keepdims=True))
    mine = jnp.concatenate(mine, axis=0)
    ids = lax.broadcasted_iota(jnp.int32, (2 * PER, total), 1).astype(F32)
    hot = jnp.where(ids == mine, 1.0, 0.0).astype(BF)
    prior = []
    for b in range(2):
        prow = jnp.zeros((1, members), F32)
        for s in range(PER):
            f = mine[b * PER + s:b * PER + s + 1, :]
            v = jnp.where(place == f, mean_ref[...], 0.0)
            v = jnp.sum(jnp.sum(v, axis=0, keepdims=True), axis=1, keepdims=True)
            prow = prow + jnp.where(lane == ny * s + ay, jnp.broadcast_to(v, (1, members)), 0.0)
        prior.append(prow)
    for b in range(2):
        hi = prior[b].astype(BF).astype(F32)
        rows[2 * b:2 * b + 1, :] = hi
        rows[2 * b + 1:2 * b + 2, :] = prior[b] - hi
    send[2] = rows[0:4, :].astype(BF)
    load.wait()
    rows[...] = mm(hot, cells[...])
    send[0] = rows[0:4, :].astype(BF)
    send[1] = rows[4:8, :].astype(BF)

    def flatten(ref, bias):
        acc = jnp.zeros((2 * nx, members), F32)
        for s in range(PER):
            spot = jnp.where(lax.broadcasted_iota(jnp.int32, (ny, members), 1)
                             == lax.broadcasted_iota(jnp.int32, (ny, members), 0) + ny * s, 1.0, 0.0)
            acc = acc + exact(ref[:, s, :].astype(F32), spot.astype(F32))
        return acc + bias

    group = lax.rem(lax.broadcasted_iota(jnp.int32, (2 * nx, members), 0), nx)
    strip = lax.rem(lax.broadcasted_iota(jnp.int32, (2 * nx, members), 1), ny)
    meta_ref[0] = flatten(col_ref, (group * cols_x).astype(F32))
    meta_ref[1] = flatten(row_ref, (strip * rows_y).astype(F32))
    meta_ref[2] = flatten(var_ref, 0.0)
    meta_ref[3] = flatten(val_ref, 0.0)

    inv_sq = 1.0 / (radius * radius)
    unit = 1.0 / (members - 1.0)
    col_x = (ax * cols_x + lax.broadcasted_iota(jnp.int32, (cols_x, 1), 0)).astype(F32)
    for b in range(2):
        ddx = col_x - wide(meta_ref[0, b * nx:(b + 1) * nx, :])
        dx2[b] = ddx * ddx * inv_sq + 1e-30
    columns(meta_ref[0, nx:2 * nx, :], xcol)
    columns(meta_ref[1, nx:2 * nx, :], ycol)

    def ship(n):
        pltpu.make_async_copy(tap.at[n], tap_ref.at[n], tap_sem).start()

    def cross_tile(i, carry):
        r = pl.ds(pl.multiple_of(i * 128, 128), 128)
        x_c, y_c = xcol[r, :], ycol[r, :]
        for c in range(nx):
            ddx = x_c - meta_ref[0, c:c + 1, :]
            ddy = y_c - meta_ref[1, c:c + 1, :]
            t = (ddx * ddx + ddy * ddy) * inv_sq + 1e-30
            tap[i, :, c * 128:(c + 1) * 128] = taper_scaled(t, unit)
        ship(i)
        return carry

    def own_tile(n, carry):
        b = n // rows_y
        here = (ay * rows_y + lax.rem(n, rows_y)).astype(F32)
        for c in range(nx):
            ddy = here - meta_ref[1, pl.ds(b * nx + c, 1), :]
            t = dx2[b, :, c * 128:(c + 1) * 128] + ddy * ddy * inv_sq
            tap[nx + n, :, c * 128:(c + 1) * 128] = taper_scaled(t, unit)
        ship(nx + n)
        return carry

    first, second, third = SPLIT
    lax.fori_loop(0, first, cross_tile, 0)
    pl.semaphore_wait(barrier, ny - 1 + nx - 1)

    own = pltpu.make_async_copy(send, near.at[:, ay], self_sem.at[0])
    own.start()

    def spread_out(o, carry):
        to = lax.rem(ay + o, ny)
        pltpu.make_async_remote_copy(
            send, near.at[:, ay], send_sem.at[to], recv_sem.at[ay],
            device_id=(ax, to), device_id_type=MESH).start()
        return carry

    lax.fori_loop(1, ny, spread_out, 0)
    lax.fori_loop(first, nx, cross_tile, 0)
    lax.fori_loop(0, second - (nx - first), own_tile, 0)
    own.wait()

    def arrive(o, carry):
        frm = lax.rem(ay + o, ny)
        pltpu.make_async_remote_copy(
            send, near.at[:, frm], send_sem.at[frm], recv_sem.at[frm],
            device_id=(ax, frm), device_id_type=MESH).wait()
        return carry

    lax.fori_loop(1, ny, arrive, 0)

    keep = pltpu.make_async_copy(near.at[0:2], allz.at[ax], self_sem.at[1])
    keep.start()

    def zout(o, carry):
        to = lax.rem(ax + 2 * o, nx)
        pltpu.make_async_remote_copy(near.at[0:2], allz.at[ax], zsend.at[to], zrecv.at[ax],
                                     device_id=(to, ay), device_id_type=MESH).start()
        return carry

    lax.fori_loop(1, nx // 2, zout, 0)
    pltpu.make_async_remote_copy(near.at[0:2], allz.at[ax], zsend.at[other], zrecv.at[ax],
                                 device_id=(other, ay), device_id_type=MESH).start()
    psum = jnp.sum(near[2].astype(F32), axis=0)
    pnear[0:1, :] = psum[0:1, :] + psum[1:2, :]
    pnear[1:2, :] = psum[2:3, :] + psum[3:4, :]
    allp[ax] = pnear[...]

    def pout(o, carry):
        to = lax.rem(ax + o, nx)
        pltpu.make_async_remote_copy(pnear, allp.at[ax], psend.at[to], precv.at[ax],
                                     device_id=(to, ay), device_id_type=MESH).start()
        return carry

    lax.fori_loop(1, nx, pout, 0)
    lax.fori_loop(second - (nx - first), second - (nx - first) + third, own_tile, 0)

    def relay(o, carry):
        g = lax.rem(ax + 2 * o, nx)
        h = g + 1 - 2 * lax.rem(g, 2)
        pltpu.make_async_remote_copy(near.at[0:2], allz.at[g], zsend.at[g], zrecv.at[g],
                                     device_id=(g, ay), device_id_type=MESH).wait()
        pltpu.make_async_remote_copy(allz.at[g], allz.at[g], zsend.at[h], zrecv.at[g],
                                     device_id=(other, ay), device_id_type=MESH).start()
        return carry

    lax.fori_loop(1, nx // 2, relay, 0)
    lax.fori_loop(second - (nx - first) + third, 2 * rows_y, own_tile, 0)

    def settle(o, carry):
        g = lax.rem(ax + 2 * o, nx)
        h = g + 1 - 2 * lax.rem(g, 2)
        pltpu.make_async_remote_copy(allz.at[h], allz.at[h], zsend.at[h], zrecv.at[h],
                                     device_id=(other, ay), device_id_type=MESH).wait()
        return carry

    lax.fori_loop(0, nx // 2, settle, 0)

    def settle_p(o, carry):
        g = lax.rem(ax + o, nx)
        pltpu.make_async_remote_copy(pnear, allp.at[g], psend.at[g], precv.at[g],
                                     device_id=(g, ay), device_id_type=MESH).wait()
        return carry

    lax.fori_loop(1, nx, settle_p, 0)
    keep.wait()
    p_ref[...] = allp[...]
    outs = [pltpu.make_async_copy(allz.at[:, b], z_ref.at[b], self_sem.at[b]) for b in range(2)]
    for c in outs:
        c.start()
    for c in outs:
        c.wait()
    pltpu.make_async_copy(tap, tap_ref, tap_sem).wait()


def gather(nx, ny, radius, cols_x, rows_y, spread, mean, col, row, lev, var, val):
    members = spread.shape[1]
    count = nx * ny * PER
    tiles = nx + 2 * rows_y
    vm = pl.BlockSpec(memory_space=pltpu.VMEM)
    hbm = pl.BlockSpec(memory_space=pl.ANY)
    dma = pltpu.SemaphoreType.DMA
    return pl.pallas_call(
        functools.partial(gather_kernel, nx, ny, radius, cols_x, rows_y),
        out_shape=(jax.ShapeDtypeStruct((2, nx, ny, PER, members), BF), jax.ShapeDtypeStruct((nx, 8, members), F32),
                   jax.ShapeDtypeStruct((4, 2 * nx, members), F32), jax.ShapeDtypeStruct((tiles, 128, count), F32)),
        in_specs=[hbm] + [vm] * 6,
        out_specs=(hbm, vm, vm, hbm),
        scratch_shapes=[
            pltpu.VMEM(spread.shape, BF),
            pltpu.VMEM((3, PER, members), BF),
            pltpu.VMEM((8, members), F32),
            pltpu.VMEM((3, ny, PER, members), BF),
            pltpu.VMEM((8, members), F32),
            pltpu.VMEM((nx, 2, ny, PER, members), BF),
            pltpu.VMEM((nx, 8, members), F32),
            pltpu.VMEM((2, cols_x, count), F32),
            pltpu.VMEM((count, members), F32),
            pltpu.VMEM((count, members), F32),
            pltpu.VMEM((tiles, 128, count), F32),
            dma, dma((2,)), dma, dma((ny,)), dma((ny,)), dma((nx,)), dma((nx,)), dma((nx,)), dma((nx,)),
        ],
        compiler_params=pltpu.CompilerParams(collective_id=0, has_side_effects=True, vmem_limit_bytes=60 << 20),
    )(spread, mean, col, row, lev, var, val)


def chain(zx, zt, qx, dcol, ivcol, z_f32, ivar_row):
    count, members = z_f32.shape
    dof = members - 1.0
    lane = lax.broadcasted_iota(jnp.int32, (count, members), 1)
    d1, d2, d3 = split3(dcol[...])
    zx[:, :members] = z_f32.astype(BF)
    zx[:, members:] = jnp.where(lane == 0, d1.astype(F32), jnp.where(
        lane == 1, d2.astype(F32), jnp.where(lane == 2, d3.astype(F32), 0.0))).astype(BF)
    z_t = z_f32.T
    zt[...] = z_t.astype(BF)
    h1, h2, h3 = split3(z_t * (ivar_row * (1.0 / dof)))
    rhs = zx[...]
    full = mm(jnp.concatenate([h1, h2, h3], axis=0), rhs)
    full = full[:members] + full[members:2 * members] + full[2 * members:]
    row_i = lax.broadcasted_iota(jnp.int32, (members, members), 0)
    col_i = lax.broadcasted_iota(jnp.int32, (members, members), 1)
    eye = jnp.where(row_i == col_i, 1.0, 0.0).astype(F32)
    gram = full[:, :members] + eye
    vec = jnp.broadcast_to(jnp.sum(full[:, members:], axis=1, keepdims=True), (members, members))
    top = jnp.max(jnp.sum(jnp.abs(gram), axis=1, keepdims=True))
    scale = 2.0 / (1.0 + top)
    first = scale * (2.0 * eye - scale * gram)

    def more(state):
        step, miss, _ = state
        return jnp.logical_and(step < 60, miss > 1e-3)

    def newton(state):
        step, _, x = state
        resid = eye - exact(gram, x)
        x = x + exact(x, resid)
        return step + 1, jnp.max(jnp.abs(resid)), x

    _, _, inv = lax.while_loop(more, newton, (jnp.int32(0), jnp.float32(1.0), first))
    w = exact(inv, vec)
    r1, r2, r3 = split3(jnp.concatenate([inv, -w], axis=1))
    row_e = lax.broadcasted_iota(jnp.int32, (members, 2 * members), 0)
    col_e = lax.broadcasted_iota(jnp.int32, (members, 2 * members), 1)
    ones = jnp.where(jnp.logical_and(row_e < 3, col_e >= members), 1.0, 0.0).astype(BF)
    z_b = rhs[:, :members]
    acc = mm(rhs, jnp.concatenate([r1, ones], axis=0)) + mm(
        jnp.concatenate([z_b, z_b], axis=1), jnp.concatenate([r2, r3], axis=0))
    iv = ivcol[...]
    qx[...] = (acc * jnp.concatenate([iv, iv], axis=1)).astype(BF)


def update_kernel(nx, ny, step_y, spread_hbm, mean_ref, z_ref, p_ref, meta_ref, tap_hbm, mean_out, spread_out,
                  spread_in, zx, zt, qx, zf, z1, dcol, ivcol, macc, gain, tap, tap_sem, in_sem):
    levels, rows_y, cols_x, members = spread_out.shape
    count = z1.shape[0]
    loads = [pltpu.make_async_copy(tap_hbm.at[0:nx], tap.at[0:nx], tap_sem.at[0])]
    for b in range(2):
        cut = slice(nx + b * rows_y, nx + (b + 1) * rows_y)
        loads.append(pltpu.make_async_copy(tap_hbm.at[cut], tap.at[cut], tap_sem.at[b + 1]))
    fetch = pltpu.make_async_copy(spread_hbm, spread_in, in_sem)
    loads[0].start()
    fetch.start()
    loads[1].start()
    loads[2].start()

    def panel(b):
        zf[...] = z_ref[b].astype(F32).reshape(count, members)
        group = ny * PER
        return jnp.concatenate([zf[pl.ds(i * group + s, ny, stride=PER), :]
                                for i in range(nx) for s in range(PER)], axis=0)

    def rows8(q, b):
        return meta_ref[q, b * nx:(b + 1) * nx, :]

    def gap(b):
        return rows8(3, b) - jnp.concatenate([p_ref[i, b:b + 1, :] for i in range(nx)], axis=0)

    columns(gap(0), dcol)
    columns(1.0 / rows8(2, 0), ivcol)
    chain(zx, zt.at[0], qx.at[0], dcol, ivcol, panel(0), wide(1.0 / rows8(2, 0)))
    columns(gap(1), dcol)
    columns(1.0 / rows8(2, 1), ivcol)
    z1[...] = panel(1).astype(BF)
    loads[0].wait()

    def cross(c, carry):
        r = pl.ds(pl.multiple_of(c * 256, 256), 256)
        z_c = z1[r, :]
        for i in range(count // 256):
            cut = slice(i * 256, (i + 1) * 256)
            cov = mm(z_c, zt[0, :, cut])
            gain[0:256, cut] = (tap[pl.ds(2 * c, 2), :, cut].reshape(256, 256) * cov).astype(BF)
        inc = mm(gain[0:256, :], qx[0])
        z1[r, :] = (z_c.astype(F32) - 0.5 * inc[:, :members]).astype(BF)
        dcol[r, :] = dcol[r, :] - inc[:, members:]
        return carry

    lax.fori_loop(0, count // 256, cross, 0)
    chain(zx, zt.at[1], qx.at[1], dcol, ivcol, z1[...].astype(F32), wide(1.0 / rows8(2, 1)))

    macc[...] = jnp.zeros_like(macc)
    lane = lax.broadcasted_iota(jnp.int32, (cols_x, members), 1)
    fetch.wait()
    part = step_y * cols_x

    for b in range(2):
        loads[b + 1].wait()
        src = spread_in if b == 0 else spread_out

        def sweep(g, carry):
            y = g * step_y
            s = src[:, pl.ds(y, step_y)].reshape(levels * part, members)
            for i in range(count // 256):
                cut = slice(i * 256, (i + 1) * 256)
                cov = mm(s, zt[b, :, cut])
                t = tap[pl.ds(nx + b * rows_y + y, step_y), :, cut].reshape(part, 256)
                for lev in range(levels):
                    gain[lev * part:(lev + 1) * part, cut] = (t * cov[lev * part:(lev + 1) * part]).astype(BF)
            inc = mm(gain[...], qx[b])
            new = (s.astype(F32) - 0.5 * inc[:, :members]).astype(BF)
            spread_out[:, pl.ds(y, step_y)] = new.reshape(levels, step_y, cols_x, members)
            acc = macc[...]
            for lev in range(levels):
                for k in range(step_y):
                    at = (lev * step_y + k) * cols_x
                    acc = acc + jnp.where(lane == lev * rows_y + y + k, inc[at:at + cols_x, members:], 0.0)
            macc[...] = acc
            return carry

        lax.fori_loop(0, rows_y // step_y, sweep, 0)
    mean_out[...] = mean_ref[...] + macc[...].T[:levels * rows_y, :]


def update(nx, ny, step_y, spread, mean, z, p, meta, tap):
    levels, rows_y, cols_x, members = spread.shape
    count = tap.shape[2]
    vm = pl.BlockSpec(memory_space=pltpu.VMEM)
    hbm = pl.BlockSpec(memory_space=pl.ANY)
    return pl.pallas_call(
        functools.partial(update_kernel, nx, ny, step_y),
        out_shape=(jax.ShapeDtypeStruct(mean.shape, F32), jax.ShapeDtypeStruct(spread.shape, BF)),
        in_specs=[hbm, vm, vm, vm, vm, hbm],
        out_specs=(vm, vm),
        scratch_shapes=[
            pltpu.VMEM(spread.shape, BF),
            pltpu.VMEM((count, 2 * members), BF),
            pltpu.VMEM((2, members, count), BF),
            pltpu.VMEM((2, count, 2 * members), BF),
            pltpu.VMEM((count, members), F32),
            pltpu.VMEM((count, members), BF),
            pltpu.VMEM((count, members), F32),
            pltpu.VMEM((count, members), F32),
            pltpu.VMEM((cols_x, members), F32),
            pltpu.VMEM((levels * step_y * cols_x, count), BF),
            pltpu.VMEM(tap.shape, F32),
            pltpu.SemaphoreType.DMA((3,)),
            pltpu.SemaphoreType.DMA,
        ],
        compiler_params=pltpu.CompilerParams(vmem_limit_bytes=60 << 20),
    )(spread, mean, z, p, meta, tap)


def body(state_mean, state_spread, obs_value, obs_var, obs_col, obs_row, obs_level):
    levels, rows_y, cols_x, members = state_spread.shape
    nx, ny = lax.axis_size("gx"), lax.axis_size("gy")
    radius = nx * cols_x // 2
    spread = state_spread.reshape(levels * rows_y * cols_x, members)
    mean = state_mean.reshape(levels * rows_y, cols_x)

    def turn(a):
        return jnp.transpose(a, (0, 1, 3, 2)).reshape(2 * nx, PER, ny)

    z, p, meta, tap = gather(nx, ny, radius, cols_x, rows_y, spread, mean, turn(obs_col), turn(obs_row),
                             turn(obs_level), turn(obs_var), turn(obs_value))
    new_mean, new_spread = update(nx, ny, 2, state_spread, mean, z, p, meta, tap)
    return new_mean.reshape(state_mean.shape), new_spread


def solution(mesh):
    return jax.shard_map(
        body,
        mesh=mesh,
        in_specs=(P(None, "gy", "gx"), P(None, "gy", "gx", None), P(), P(), P(), P(), P()),
        out_specs=(P(None, "gy", "gx"), P(None, "gy", "gx", None)),
        check_vma=False,
    )
```

time: 71.4 us -> 59.3 us (0.83)
  Pallas kernels: 67 us -> 58.7 us
  local copies, waits for them, and re-layouts: 2.68 us -> 0 us
  other arithmetic: 0.92 us -> 0 us
    pallas_call x2, Pallas kernels: 67 us -> 58.7 us  [the longest x1 30.8 us: gather(): pl.pallas_call(functools.partial(gather_kernel, nx, ny, radius, cols_x, r...]
    reshape x2 -> x0, local copies, waits for them, and re-layouts: 2.03 us -> none  [the longest x1 1.27 us: body(): meta = jnp.stack([obs_x, obs_y, obs_var, obs_value], axis=1).reshape(8, -1)]
    another operation x2 -> x0, other arithmetic: 0.92 us -> none  [body(): meta = jnp.stack([obs_x, obs_y, obs_var, obs_value], axis=1).reshape(8, -1)]
where the time goes in v2:
time: 59.3 us
  Pallas kernels  58.7 us (99%)
  between operations  0.64 us (1%)
    pallas_call x1, Pallas kernels, gather(): pl.pallas_call(functools.partial(gather_kernel, nx, ny, radius, cols_x, r...  30.8 us
    pallas_call x1, Pallas kernels, update(): pl.pallas_call(functools.partial(update_kernel, nx, ny, step_y), out_shap...  27.9 us

profile of v2, /device:TPU:1, one launch (start us, length us, event | category | flops | bytes accessed | tf_op | source)
XLA Modules:
  0.0 59.3 jit_solution(16154385686247539603)
XLA Ops:
  0.6 30.8 %shard_map.86 = (bf16[2,8,32,4,128]{4,3,2,1,0:T(4,128)(2,1)}, f32[8,8,128]{2,1,0:T(8,128)}, f32[4,16,128]{2,1,0:T(8,128)}, f32[40,128,1024]{2,1,0:T(8,128)}) custom-call(bf16[4096,128]{1,0:T(8,128)(2,1)} %bitcast.18, f32[32,128]{1,0:T(8,128)} %bitcast.19, s32[16,4,32]{2,1,0:T(4,128)} %bitcast.21, s32[16,4,32]{2,1,0:T(4,128)} %bitcast.22, ...), custom_call_target="tpu_custom_call" | custom-call | tf_op jit(solution)/shard_map/pallas_call | solution.py:257
  31.4 27.9 %shard_map.87 = (f32[32,128]{1,0:T(8,128)}, bf16[2,16,128,128]{3,2,1,0:T(8,128)(2,1)}) custom-call(bf16[2,16,128,128]{3,2,1,0:T(8,128)(2,1)} %spread_hbm.1, f32[32,128]{1,0:T(8,128)} %bitcast.20, bf16[2,8,32,4,128]{4,3,2,1,0:T(4,128)(2,1)} %get-tuple-element.8.z_ref, f32[8,8,128]{2,1,0:T(8,128)} %get-tuple-element.9.p_ref, ...), custom_call_target="tpu_custom_call" | custom-call | tf_op jit(solution)/shard_map/pallas_call | solution.py:414

commit v3 on v2

--- a/solution.py
+++ b/solution.py
@@ -10,8 +10,10 @@
 HI = lax.Precision.HIGHEST
 BF = jnp.bfloat16
 F32 = jnp.float32
+DOUBLINGS = 3
+STEP_Y = 4
 PER = 4
-SPLIT = (4, 20, 12)
+SPLIT = (6, 6)
 
 
 def mm(a, b):
@@ -29,15 +31,19 @@
     return a, b, (r - b.astype(F32)).astype(BF)
 
 
-def taper_scaled(t, c):
-    rs = lax.rsqrt(t)
-    r = t * rs
-    inner = (((-0.25 * c * r + 0.5 * c) * r + 0.625 * c) * r - 5.0 / 3.0 * c) * t + c
-    m = jnp.maximum(2.0 - r, 0.0)
+def taper_scale(members):
+    return (0.25 / (members - 1.0)) ** 0.2
+
+
+def taper(sq, lam):
+    rs = lax.rsqrt(sq)
+    r = sq * rs
+    inner = (((r - 2.0 * lam) * r - 2.5 * lam ** 2) * r + 20.0 / 3.0 * lam ** 3) * sq - 4.0 * lam ** 5
+    m = jnp.maximum(2.0 * lam - r, 0.0)
     m = m * m
     m = m * m
-    outer = m * ((r * (c / 12.0) + c / 6.0) - rs * (c / 24.0))
-    return jnp.where(t <= 1.0, inner, outer)
+    outer = m * (rs * (lam ** 2 / 6.0) - (r * (1.0 / 3.0) + 2.0 / 3.0 * lam))
+    return jnp.minimum(inner, outer)
 
 
 def columns(rows8, out):
@@ -50,14 +56,17 @@
     return jnp.concatenate([rows8[i:i + 1, :] for i in range(8)], axis=1)
 
 
-def gather_kernel(nx, ny, radius, cols_x, rows_y, spread_hbm, mean_ref, col_ref, row_ref, lev_ref, var_ref, val_ref,
-                  z_ref, p_ref, meta_ref, tap_ref,
-                  cells, send, rows, near, pnear, allz, allp, dx2, xcol, ycol, tap,
-                  load_sem, self_sem, tap_sem, send_sem, recv_sem, zsend, zrecv, psend, precv):
+def gather_kernel(nx, ny, radius, cols_x, rows_y, spread_hbm, mean_hbm, col_hbm, row_hbm, lev_hbm, var_hbm, val_hbm,
+                  z_ref, p_ref, meta_ref, tap_ref, cells, mean_ref,
+                  col_ref, row_ref, lev_ref, var_ref, val_ref, send, rows, near, pnear, allz, allp, dx2, xcol, ycol,
+                  load_sem, self_sem, send_sem, recv_sem, zsend, zrecv, psend, precv):
     ax = lax.axis_index("gx")
     ay = lax.axis_index("gy")
-    load = pltpu.make_async_copy(spread_hbm, cells, load_sem)
-    load.start()
+    pairs = ((col_hbm, col_ref), (row_hbm, row_ref), (lev_hbm, lev_ref), (mean_hbm, mean_ref),
+             (spread_hbm, cells), (var_hbm, var_ref), (val_hbm, val_ref))
+    loads = [pltpu.make_async_copy(src, dst, load_sem.at[n]) for n, (src, dst) in enumerate(pairs)]
+    for load in loads:
+        load.start()
     other = ax + 1 - 2 * lax.rem(ax, 2)
     barrier = pltpu.get_barrier_semaphore()
 
@@ -79,6 +88,8 @@
     place = (lax.broadcasted_iota(jnp.int32, mean_ref.shape, 0) * cols_x
              + lax.broadcasted_iota(jnp.int32, mean_ref.shape, 1)).astype(F32)
 
+    for load in loads[:4]:
+        load.wait()
     mine = []
     for b in range(2):
         at = b * nx + ax
@@ -102,10 +113,26 @@
         rows[2 * b:2 * b + 1, :] = hi
         rows[2 * b + 1:2 * b + 2, :] = prior[b] - hi
     send[2] = rows[0:4, :].astype(BF)
-    load.wait()
+    loads[4].wait()
     rows[...] = mm(hot, cells[...])
     send[0] = rows[0:4, :].astype(BF)
     send[1] = rows[4:8, :].astype(BF)
+
+    pl.semaphore_wait(barrier, ny - 1 + nx - 1)
+
+    own = pltpu.make_async_copy(send, near.at[:, ay], self_sem.at[0])
+    own.start()
+
+    def spread_out(o, carry):
+        to = lax.rem(ay + o, ny)
+        pltpu.make_async_remote_copy(
+            send, near.at[:, ay], send_sem.at[to], recv_sem.at[ay],
+            device_id=(ax, to), device_id_type=MESH).start()
+        return carry
+
+    lax.fori_loop(1, ny, spread_out, 0)
+    loads[5].wait()
+    loads[6].wait()
 
     def flatten(ref, bias):
         acc = jnp.zeros((2 * nx, members), F32)
@@ -122,17 +149,13 @@
     meta_ref[2] = flatten(var_ref, 0.0)
     meta_ref[3] = flatten(val_ref, 0.0)
 
-    inv_sq = 1.0 / (radius * radius)
-    unit = 1.0 / (members - 1.0)
+    lam = taper_scale(members)
+    inv_sq = (lam / radius) ** 2
     col_x = (ax * cols_x + lax.broadcasted_iota(jnp.int32, (cols_x, 1), 0)).astype(F32)
-    for b in range(2):
-        ddx = col_x - wide(meta_ref[0, b * nx:(b + 1) * nx, :])
-        dx2[b] = ddx * ddx * inv_sq + 1e-30
+    ddx = col_x - wide(meta_ref[0, 0:nx, :])
+    dx2[...] = ddx * ddx * inv_sq + 1e-30
     columns(meta_ref[0, nx:2 * nx, :], xcol)
     columns(meta_ref[1, nx:2 * nx, :], ycol)
-
-    def ship(n):
-        pltpu.make_async_copy(tap.at[n], tap_ref.at[n], tap_sem).start()
 
     def cross_tile(i, carry):
         r = pl.ds(pl.multiple_of(i * 128, 128), 128)
@@ -141,37 +164,20 @@
             ddx = x_c - meta_ref[0, c:c + 1, :]
             ddy = y_c - meta_ref[1, c:c + 1, :]
             t = (ddx * ddx + ddy * ddy) * inv_sq + 1e-30
-            tap[i, :, c * 128:(c + 1) * 128] = taper_scaled(t, unit)
-        ship(i)
+            tap_ref[i, :, c * 128:(c + 1) * 128] = taper(t, lam)
         return carry
 
     def own_tile(n, carry):
-        b = n // rows_y
-        here = (ay * rows_y + lax.rem(n, rows_y)).astype(F32)
+        here = (ay * rows_y + n).astype(F32)
         for c in range(nx):
-            ddy = here - meta_ref[1, pl.ds(b * nx + c, 1), :]
-            t = dx2[b, :, c * 128:(c + 1) * 128] + ddy * ddy * inv_sq
-            tap[nx + n, :, c * 128:(c + 1) * 128] = taper_scaled(t, unit)
-        ship(nx + n)
-        return carry
-
-    first, second, third = SPLIT
-    lax.fori_loop(0, first, cross_tile, 0)
-    pl.semaphore_wait(barrier, ny - 1 + nx - 1)
-
-    own = pltpu.make_async_copy(send, near.at[:, ay], self_sem.at[0])
-    own.start()
-
-    def spread_out(o, carry):
-        to = lax.rem(ay + o, ny)
-        pltpu.make_async_remote_copy(
-            send, near.at[:, ay], send_sem.at[to], recv_sem.at[ay],
-            device_id=(ax, to), device_id_type=MESH).start()
-        return carry
-
-    lax.fori_loop(1, ny, spread_out, 0)
-    lax.fori_loop(first, nx, cross_tile, 0)
-    lax.fori_loop(0, second - (nx - first), own_tile, 0)
+            ddy = here - meta_ref[1, c:c + 1, :]
+            t = dx2[:, c * 128:(c + 1) * 128] + ddy * ddy * inv_sq
+            tap_ref[nx + n, :, c * 128:(c + 1) * 128] = taper(t, lam)
+        return carry
+
+    first, second = SPLIT
+    lax.fori_loop(0, nx, cross_tile, 0)
+    lax.fori_loop(0, first, own_tile, 0)
     own.wait()
 
     def arrive(o, carry):
@@ -207,7 +213,7 @@
         return carry
 
     lax.fori_loop(1, nx, pout, 0)
-    lax.fori_loop(second - (nx - first), second - (nx - first) + third, own_tile, 0)
+    lax.fori_loop(first, first + second, own_tile, 0)
 
     def relay(o, carry):
         g = lax.rem(ax + 2 * o, nx)
@@ -219,7 +225,7 @@
         return carry
 
     lax.fori_loop(1, nx // 2, relay, 0)
-    lax.fori_loop(second - (nx - first) + third, 2 * rows_y, own_tile, 0)
+    lax.fori_loop(first + second, rows_y, own_tile, 0)
 
     def settle(o, carry):
         g = lax.rem(ax + 2 * o, nx)
@@ -239,43 +245,43 @@
     lax.fori_loop(1, nx, settle_p, 0)
     keep.wait()
     p_ref[...] = allp[...]
-    outs = [pltpu.make_async_copy(allz.at[:, b], z_ref.at[b], self_sem.at[b]) for b in range(2)]
-    for c in outs:
-        c.start()
-    for c in outs:
-        c.wait()
-    pltpu.make_async_copy(tap, tap_ref, tap_sem).wait()
+    for b in range(2):
+        z_ref[b] = allz[:, b]
 
 
 def gather(nx, ny, radius, cols_x, rows_y, spread, mean, col, row, lev, var, val):
     members = spread.shape[1]
     count = nx * ny * PER
-    tiles = nx + 2 * rows_y
+    tiles = nx + rows_y
     vm = pl.BlockSpec(memory_space=pltpu.VMEM)
-    hbm = pl.BlockSpec(memory_space=pl.ANY)
+    hbm = pl.BlockSpec(memory_space=pltpu.HBM)
     dma = pltpu.SemaphoreType.DMA
     return pl.pallas_call(
         functools.partial(gather_kernel, nx, ny, radius, cols_x, rows_y),
-        out_shape=(jax.ShapeDtypeStruct((2, nx, ny, PER, members), BF), jax.ShapeDtypeStruct((nx, 8, members), F32),
-                   jax.ShapeDtypeStruct((4, 2 * nx, members), F32), jax.ShapeDtypeStruct((tiles, 128, count), F32)),
-        in_specs=[hbm] + [vm] * 6,
-        out_specs=(hbm, vm, vm, hbm),
+        out_shape=(pltpu.VMEM((2, nx, ny, PER, members), BF), pltpu.VMEM((nx, 8, members), F32),
+                   pltpu.VMEM((4, 2 * nx, members), F32), pltpu.VMEM((tiles, 128, count), F32),
+                   pltpu.VMEM(spread.shape, BF), pltpu.VMEM(mean.shape, F32)),
+        in_specs=[hbm] * 7,
+        out_specs=(vm,) * 6,
         scratch_shapes=[
-            pltpu.VMEM(spread.shape, BF),
+            pltpu.VMEM(col.shape, jnp.int32),
+            pltpu.VMEM(col.shape, jnp.int32),
+            pltpu.VMEM(col.shape, jnp.int32),
+            pltpu.VMEM(col.shape, F32),
+            pltpu.VMEM(col.shape, F32),
             pltpu.VMEM((3, PER, members), BF),
             pltpu.VMEM((8, members), F32),
             pltpu.VMEM((3, ny, PER, members), BF),
             pltpu.VMEM((8, members), F32),
             pltpu.VMEM((nx, 2, ny, PER, members), BF),
             pltpu.VMEM((nx, 8, members), F32),
-            pltpu.VMEM((2, cols_x, count), F32),
+            pltpu.VMEM((cols_x, count), F32),
             pltpu.VMEM((count, members), F32),
             pltpu.VMEM((count, members), F32),
-            pltpu.VMEM((tiles, 128, count), F32),
-            dma, dma((2,)), dma, dma((ny,)), dma((ny,)), dma((nx,)), dma((nx,)), dma((nx,)), dma((nx,)),
+            dma((7,)), dma((2,)), dma((ny,)), dma((ny,)), dma((nx,)), dma((nx,)), dma((nx,)), dma((nx,)),
         ],
-        compiler_params=pltpu.CompilerParams(collective_id=0, has_side_effects=True, vmem_limit_bytes=60 << 20),
-    )(spread, mean, col, row, lev, var, val)
+        compiler_params=pltpu.CompilerParams(collective_id=0, has_side_effects=True, vmem_limit_bytes=20 << 20),
+    )(*[pltpu.with_memory_space_constraint(a, pltpu.HBM) for a in (spread, mean, col, row, lev, var, val)])
 
 
 def chain(zx, zt, qx, dcol, ivcol, z_f32, ivar_row):
@@ -297,21 +303,29 @@
     eye = jnp.where(row_i == col_i, 1.0, 0.0).astype(F32)
     gram = full[:, :members] + eye
     vec = jnp.broadcast_to(jnp.sum(full[:, members:], axis=1, keepdims=True), (members, members))
-    top = jnp.max(jnp.sum(jnp.abs(gram), axis=1, keepdims=True))
+
+    square = exact(gram, gram)
+    top = jnp.sqrt(jnp.max(jnp.sum(jnp.abs(square), axis=1, keepdims=True), axis=0, keepdims=True))
     scale = 2.0 / (1.0 + top)
-    first = scale * (2.0 * eye - scale * gram)
+    resid = eye - 2.0 * scale * gram + scale * scale * square
+    inv = scale * (2.0 * eye - scale * gram)
+    for _ in range(DOUBLINGS):
+        both = exact(jnp.concatenate([inv, resid], axis=0), resid)
+        inv = inv + both[:members]
+        resid = both[members:]
+    inv = inv + exact(inv, resid)
 
     def more(state):
         step, miss, _ = state
-        return jnp.logical_and(step < 60, miss > 1e-3)
+        return jnp.logical_and(step < 60, miss > 1e-2)
 
     def newton(state):
         step, _, x = state
         resid = eye - exact(gram, x)
         x = x + exact(x, resid)
-        return step + 1, jnp.max(jnp.abs(resid)), x
-
-    _, _, inv = lax.while_loop(more, newton, (jnp.int32(0), jnp.float32(1.0), first))
+        return step + 1, jnp.max(jnp.sum(jnp.abs(resid), axis=1, keepdims=True)), x
+
+    _, _, inv = lax.while_loop(more, newton, (jnp.int32(0), jnp.float32(1.0), inv))
     w = exact(inv, vec)
     r1, r2, r3 = split3(jnp.concatenate([inv, -w], axis=1))
     row_e = lax.broadcasted_iota(jnp.int32, (members, 2 * members), 0)
@@ -324,19 +338,11 @@
     qx[...] = (acc * jnp.concatenate([iv, iv], axis=1)).astype(BF)
 
 
-def update_kernel(nx, ny, step_y, spread_hbm, mean_ref, z_ref, p_ref, meta_ref, tap_hbm, mean_out, spread_out,
-                  spread_in, zx, zt, qx, zf, z1, dcol, ivcol, macc, gain, tap, tap_sem, in_sem):
+def update_kernel(nx, ny, radius, step_y, spread_ref, mean_ref, z_ref, p_ref, meta_ref, tap, mean_out, spread_hbm,
+                  spread_out, out_sem, zx, zt, qx, zf, z1, dcol, ivcol, macc, gain, dx2, ahead):
     levels, rows_y, cols_x, members = spread_out.shape
     count = z1.shape[0]
-    loads = [pltpu.make_async_copy(tap_hbm.at[0:nx], tap.at[0:nx], tap_sem.at[0])]
-    for b in range(2):
-        cut = slice(nx + b * rows_y, nx + (b + 1) * rows_y)
-        loads.append(pltpu.make_async_copy(tap_hbm.at[cut], tap.at[cut], tap_sem.at[b + 1]))
-    fetch = pltpu.make_async_copy(spread_hbm, spread_in, in_sem)
-    loads[0].start()
-    fetch.start()
-    loads[1].start()
-    loads[2].start()
+    unit = -1.0
 
     def panel(b):
         zf[...] = z_ref[b].astype(F32).reshape(count, members)
@@ -356,31 +362,42 @@
     columns(gap(1), dcol)
     columns(1.0 / rows8(2, 1), ivcol)
     z1[...] = panel(1).astype(BF)
-    loads[0].wait()
 
     def cross(c, carry):
-        r = pl.ds(pl.multiple_of(c * 256, 256), 256)
+        r = pl.ds(pl.multiple_of(c * 512, 512), 512)
         z_c = z1[r, :]
         for i in range(count // 256):
             cut = slice(i * 256, (i + 1) * 256)
             cov = mm(z_c, zt[0, :, cut])
-            gain[0:256, cut] = (tap[pl.ds(2 * c, 2), :, cut].reshape(256, 256) * cov).astype(BF)
-        inc = mm(gain[0:256, :], qx[0])
-        z1[r, :] = (z_c.astype(F32) - 0.5 * inc[:, :members]).astype(BF)
-        dcol[r, :] = dcol[r, :] - inc[:, members:]
-        return carry
-
-    lax.fori_loop(0, count // 256, cross, 0)
+            gain[0:512, cut] = (tap[pl.ds(4 * c, 4), :, cut].reshape(512, 256) * cov).astype(BF)
+        inc = mm(gain[0:512, :], qx[0])
+        z1[r, :] = (z_c.astype(F32) - (0.5 * unit) * inc[:, :members]).astype(BF)
+        dcol[r, :] = dcol[r, :] - unit * inc[:, members:]
+        return carry
+
+    lax.fori_loop(0, count // 512, cross, 0)
     chain(zx, zt.at[1], qx.at[1], dcol, ivcol, z1[...].astype(F32), wide(1.0 / rows8(2, 1)))
 
     macc[...] = jnp.zeros_like(macc)
     lane = lax.broadcasted_iota(jnp.int32, (cols_x, members), 1)
-    fetch.wait()
     part = step_y * cols_x
+    half = step_y // 2
+    lam = taper_scale(members)
+    inv_sq = (lam / radius) ** 2
+    col_x = (lax.axis_index("gx") * cols_x + lax.broadcasted_iota(jnp.int32, (cols_x, 1), 0)).astype(F32)
+    ddx = col_x - wide(meta_ref[0, nx:2 * nx, :])
+    dx2[...] = ddx * ddx * inv_sq + 1e-30
+    base_y = lax.axis_index("gy") * rows_y
+
+    def taper_rows(y, cut):
+        out = []
+        for c in range(cut.start // 128, cut.stop // 128):
+            ddy = (base_y + y).astype(F32) - meta_ref[1, nx + c:nx + c + 1, :]
+            out.append(taper(dx2[:, c * 128:(c + 1) * 128] + ddy * ddy * inv_sq, lam))
+        return jnp.concatenate(out, axis=1)
 
     for b in range(2):
-        loads[b + 1].wait()
-        src = spread_in if b == 0 else spread_out
+        src = spread_ref if b == 0 else spread_out
 
         def sweep(g, carry):
             y = g * step_y
@@ -388,12 +405,21 @@
             for i in range(count // 256):
                 cut = slice(i * 256, (i + 1) * 256)
                 cov = mm(s, zt[b, :, cut])
-                t = tap[pl.ds(nx + b * rows_y + y, step_y), :, cut].reshape(part, 256)
+                if b == 0:
+                    t = tap[pl.ds(nx + y, step_y), :, cut].reshape(part, 256)
+                    for k in range(half):
+                        ahead[g * half + k, :, cut] = taper_rows(y + k, cut)
+                else:
+                    t = jnp.concatenate([ahead[g * half + k, :, cut] for k in range(half)]
+                                        + [taper_rows(y + k, cut) for k in range(half, step_y)], axis=0)
                 for lev in range(levels):
                     gain[lev * part:(lev + 1) * part, cut] = (t * cov[lev * part:(lev + 1) * part]).astype(BF)
             inc = mm(gain[...], qx[b])
-            new = (s.astype(F32) - 0.5 * inc[:, :members]).astype(BF)
+            new = (s.astype(F32) - (0.5 * unit) * inc[:, :members]).astype(BF)
             spread_out[:, pl.ds(y, step_y)] = new.reshape(levels, step_y, cols_x, members)
+            if b == 1:
+                pltpu.make_async_copy(spread_out.at[:, pl.ds(y, step_y)], spread_hbm.at[:, pl.ds(y, step_y)],
+                                      out_sem).start()
             acc = macc[...]
             for lev in range(levels):
                 for k in range(step_y):
@@ -403,21 +429,22 @@
             return carry
 
         lax.fori_loop(0, rows_y // step_y, sweep, 0)
-    mean_out[...] = mean_ref[...] + macc[...].T[:levels * rows_y, :]
-
-
-def update(nx, ny, step_y, spread, mean, z, p, meta, tap):
+    pltpu.make_async_copy(spread_out, spread_hbm, out_sem).wait()
+    mean_out[...] = mean_ref[...] + unit * macc[...].T[:levels * rows_y, :]
+
+
+def update(nx, ny, radius, step_y, spread, mean, z, p, meta, tap):
     levels, rows_y, cols_x, members = spread.shape
     count = tap.shape[2]
     vm = pl.BlockSpec(memory_space=pltpu.VMEM)
-    hbm = pl.BlockSpec(memory_space=pl.ANY)
     return pl.pallas_call(
-        functools.partial(update_kernel, nx, ny, step_y),
+        functools.partial(update_kernel, nx, ny, radius, step_y),
         out_shape=(jax.ShapeDtypeStruct(mean.shape, F32), jax.ShapeDtypeStruct(spread.shape, BF)),
-        in_specs=[hbm, vm, vm, vm, vm, hbm],
-        out_specs=(vm, vm),
+        in_specs=[vm] * 6,
+        out_specs=(vm, pl.BlockSpec(memory_space=pltpu.HBM)),
         scratch_shapes=[
             pltpu.VMEM(spread.shape, BF),
+            pltpu.SemaphoreType.DMA,
             pltpu.VMEM((count, 2 * members), BF),
             pltpu.VMEM((2, members, count), BF),
             pltpu.VMEM((2, count, 2 * members), BF),
@@ -427,11 +454,10 @@
             pltpu.VMEM((count, members), F32),
             pltpu.VMEM((cols_x, members), F32),
             pltpu.VMEM((levels * step_y * cols_x, count), BF),
-            pltpu.VMEM(tap.shape, F32),
-            pltpu.SemaphoreType.DMA((3,)),
-            pltpu.SemaphoreType.DMA,
+            pltpu.VMEM((cols_x, count), F32),
+            pltpu.VMEM((rows_y // 2, cols_x, count), F32),
         ],
-        compiler_params=pltpu.CompilerParams(vmem_limit_bytes=60 << 20),
+        compiler_params=pltpu.CompilerParams(vmem_limit_bytes=34 << 20),
     )(spread, mean, z, p, meta, tap)
 
 
@@ -445,9 +471,9 @@
     def turn(a):
         return jnp.transpose(a, (0, 1, 3, 2)).reshape(2 * nx, PER, ny)
 
-    z, p, meta, tap = gather(nx, ny, radius, cols_x, rows_y, spread, mean, turn(obs_col), turn(obs_row),
+    z, p, meta, tap, cells, mean = gather(nx, ny, radius, cols_x, rows_y, spread, mean, turn(obs_col), turn(obs_row),
                              turn(obs_level), turn(obs_var), turn(obs_value))
-    new_mean, new_spread = update(nx, ny, 2, state_spread, mean, z, p, meta, tap)
+    new_mean, new_spread = update(nx, ny, radius, STEP_Y, cells.reshape(state_spread.shape), mean, z, p, meta, tap)
     return new_mean.reshape(state_mean.shape), new_spread
 
 

time: 59.3 us -> 55.8 us (0.941)
  Pallas kernels: 58.7 us -> 55.3 us
    pallas_call x1, Pallas kernels: 30.8 us -> 27.4 us  [gather(): pl.pallas_call(functools.partial(gather_kernel, nx, ny, radius, cols_x, r...]
where the time goes in v3:
time: 55.8 us; the launch traced here: 55.9 us
  Pallas kernels  55.3 us (99%)
  between operations  0.64 us (1%)
    pallas_call x1, Pallas kernels, update(): pl.pallas_call(functools.partial(update_kernel, nx, ny, radius, step_y),...  27.9 us
    pallas_call x1, Pallas kernels, gather(): pl.pallas_call(functools.partial(gather_kernel, nx, ny, radius, cols_x, r...  27.4 us

profile of v3, /device:TPU:1, one launch (start us, length us, event | category | flops | bytes accessed | tf_op | source)
XLA Modules:
  0.0 55.9 jit_solution(14967692093317170110)
XLA Ops:
  0.6 27.4 %shard_map.86 = (bf16[2,8,32,4,128]{4,3,2,1,0:T(4,128)(2,1)S(1)}, f32[8,8,128]{2,1,0:T(8,128)S(1)}, f32[4,16,128]{2,1,0:T(8,128)S(1)}, f32[24,128,1024]{2,1,0:T(...) custom-call(bf16[4096,128]{1,0:T(8,128)(2,1)} %bitcast.20, f32[32,128]{1,0:T(8,128)} %bitcast.26, ...), custom_call_target="tpu_custom_call" | custom-call | tf_op jit(solution)/shard_map/pallas_call | solution.py:259
  28.0 27.9 %shard_map.87 = (f32[32,128]{1,0:T(8,128)}, bf16[2,16,128,128]{3,2,1,0:T(8,128)(2,1)}) custom-call(bf16[2,16,128,128]{3,2,1,0:T(8,128)(2,1)S(1)} %bitcast.19, f32[32,128]{1,0:T(8,128)S(1)} %get-tuple-element.11.mean_ref, bf16[2,8,32,4,128]{4,3,2,1,0:T(4,128)(2,1)S(1)} %get-tuple-element.12.z_ref, f32[8,8,128]{2,1,0:T(8,128)S(1)} %get-tuple-element.13.p_ref, ...), custom_call_target="tpu_custom_call" | custom-call | tf_op jit(solution)/shard_map/pallas_call | solution.py:440

commit v4 on v3

--- a/solution.py
+++ b/solution.py
@@ -11,7 +11,8 @@
 BF = jnp.bfloat16
 F32 = jnp.float32
 DOUBLINGS = 3
-STEP_Y = 4
+STEP_Y = 2
+LEAD = 2
 PER = 4
 SPLIT = (6, 6)
 
@@ -369,8 +370,8 @@
         for i in range(count // 256):
             cut = slice(i * 256, (i + 1) * 256)
             cov = mm(z_c, zt[0, :, cut])
-            gain[0:512, cut] = (tap[pl.ds(4 * c, 4), :, cut].reshape(512, 256) * cov).astype(BF)
-        inc = mm(gain[0:512, :], qx[0])
+            gain[0, 0:512, cut] = (tap[pl.ds(4 * c, 4), :, cut].reshape(512, 256) * cov).astype(BF)
+        inc = mm(gain[0, 0:512, :], qx[0])
         z1[r, :] = (z_c.astype(F32) - (0.5 * unit) * inc[:, :members]).astype(BF)
         dcol[r, :] = dcol[r, :] - unit * inc[:, members:]
         return carry
@@ -381,7 +382,6 @@
     macc[...] = jnp.zeros_like(macc)
     lane = lax.broadcasted_iota(jnp.int32, (cols_x, members), 1)
     part = step_y * cols_x
-    half = step_y // 2
     lam = taper_scale(members)
     inv_sq = (lam / radius) ** 2
     col_x = (lax.axis_index("gx") * cols_x + lax.broadcasted_iota(jnp.int32, (cols_x, 1), 0)).astype(F32)
@@ -396,39 +396,58 @@
             out.append(taper(dx2[:, c * 128:(c + 1) * 128] + ddy * ddy * inv_sq, lam))
         return jnp.concatenate(out, axis=1)
 
-    for b in range(2):
-        src = spread_ref if b == 0 else spread_out
-
-        def sweep(g, carry):
-            y = g * step_y
-            s = src[:, pl.ds(y, step_y)].reshape(levels * part, members)
-            for i in range(count // 256):
-                cut = slice(i * 256, (i + 1) * 256)
-                cov = mm(s, zt[b, :, cut])
-                if b == 0:
-                    t = tap[pl.ds(nx + y, step_y), :, cut].reshape(part, 256)
-                    for k in range(half):
-                        ahead[g * half + k, :, cut] = taper_rows(y + k, cut)
-                else:
-                    t = jnp.concatenate([ahead[g * half + k, :, cut] for k in range(half)]
-                                        + [taper_rows(y + k, cut) for k in range(half, step_y)], axis=0)
-                for lev in range(levels):
-                    gain[lev * part:(lev + 1) * part, cut] = (t * cov[lev * part:(lev + 1) * part]).astype(BF)
-            inc = mm(gain[...], qx[b])
-            new = (s.astype(F32) - (0.5 * unit) * inc[:, :members]).astype(BF)
-            spread_out[:, pl.ds(y, step_y)] = new.reshape(levels, step_y, cols_x, members)
-            if b == 1:
-                pltpu.make_async_copy(spread_out.at[:, pl.ds(y, step_y)], spread_hbm.at[:, pl.ds(y, step_y)],
-                                      out_sem).start()
-            acc = macc[...]
+    steps = rows_y // step_y
+
+    def rows_of(n):
+        return slice((n % steps) * step_y, (n % steps + 1) * step_y)
+
+    def spread_at(n):
+        ref = spread_ref if n < steps else spread_out
+        return ref[:, rows_of(n)].reshape(levels * part, members)
+
+    def fill(n):
+        b, y = n // steps, (n % steps) * step_y
+        slot = gain.at[n % 2]
+        s = spread_at(n)
+        for i in range(count // 256):
+            cut = slice(i * 256, (i + 1) * 256)
+            cov = mm(s, zt[b, :, cut])
+            if b == 0:
+                t = tap[nx + y:nx + y + step_y, :, cut].reshape(part, 256)
+            else:
+                t = ahead[y:y + step_y, :, cut].reshape(part, 256)
             for lev in range(levels):
-                for k in range(step_y):
-                    at = (lev * step_y + k) * cols_x
-                    acc = acc + jnp.where(lane == lev * rows_y + y + k, inc[at:at + cols_x, members:], 0.0)
-            macc[...] = acc
-            return carry
-
-        lax.fori_loop(0, rows_y // step_y, sweep, 0)
+                slot[lev * part:(lev + 1) * part, cut] = (t * cov[lev * part:(lev + 1) * part]).astype(BF)
+
+    def drain(n):
+        b, y = n // steps, (n % steps) * step_y
+        inc = mm(gain[n % 2], qx[b])
+        new = (spread_at(n).astype(F32) - (0.5 * unit) * inc[:, :members]).astype(BF)
+        spread_out[:, rows_of(n)] = new.reshape(levels, step_y, cols_x, members)
+        if b == 1:
+            pltpu.make_async_copy(spread_out.at[:, rows_of(n)], spread_hbm.at[:, rows_of(n)], out_sem).start()
+        acc = macc[...]
+        for lev in range(levels):
+            for k in range(step_y):
+                at = (lev * step_y + k) * cols_x
+                acc = acc + jnp.where(lane == lev * rows_y + y + k, inc[at:at + cols_x, members:], 0.0)
+        macc[...] = acc
+
+    def look_ahead(y):
+        for i in range(count // 256):
+            cut = slice(i * 256, (i + 1) * 256)
+            ahead[y, :, cut] = taper_rows(jnp.int32(y), cut)
+
+    done = 0
+    for n in range(2 * steps + 1):
+        if n > 0:
+            drain(n - 1)
+        if n < 2 * steps:
+            fill(n)
+        goal = min(rows_y, LEAD + (n + 1) * rows_y // (2 * steps))
+        for y in range(done, goal):
+            look_ahead(y)
+        done = goal
     pltpu.make_async_copy(spread_out, spread_hbm, out_sem).wait()
     mean_out[...] = mean_ref[...] + unit * macc[...].T[:levels * rows_y, :]
 
@@ -453,9 +472,9 @@
             pltpu.VMEM((count, members), F32),
             pltpu.VMEM((count, members), F32),
             pltpu.VMEM((cols_x, members), F32),
-            pltpu.VMEM((levels * step_y * cols_x, count), BF),
+            pltpu.VMEM((2, levels * step_y * cols_x, count), BF),
             pltpu.VMEM((cols_x, count), F32),
-            pltpu.VMEM((rows_y // 2, cols_x, count), F32),
+            pltpu.VMEM((rows_y, cols_x, count), F32),
         ],
         compiler_params=pltpu.CompilerParams(vmem_limit_bytes=34 << 20),
     )(spread, mean, z, p, meta, tap)

time: 55.8 us -> 52.5 us (0.941)
  Pallas kernels: 55.3 us -> 51.6 us
    pallas_call x1, Pallas kernels: 27.9 us -> 24.2 us  [update(): pl.pallas_call(functools.partial(update_kernel, nx, ny, radius, step_y),...]
where the time goes in v4:
time: 52.5 us; the launch traced here: 52.4 us
  Pallas kernels  51.6 us (98%)
  between operations  0.8 us (2%)
    pallas_call x1, Pallas kernels, gather(): pl.pallas_call(functools.partial(gather_kernel, nx, ny, radius, cols_x, r...  27.4 us
    pallas_call x1, Pallas kernels, update(): pl.pallas_call(functools.partial(update_kernel, nx, ny, radius, step_y),...  24.2 us

profile of v4, /device:TPU:1, one launch (start us, length us, event | category | flops | bytes accessed | tf_op | source)
XLA Modules:
  0.0 52.4 jit_solution(11971244399450285074)
XLA Ops:
  0.6 27.4 %shard_map.86 = (bf16[2,8,32,4,128]{4,3,2,1,0:T(4,128)(2,1)S(1)}, f32[8,8,128]{2,1,0:T(8,128)S(1)}, f32[4,16,128]{2,1,0:T(8,128)S(1)}, f32[24,128,1024]{2,1,0:T(...) custom-call(bf16[4096,128]{1,0:T(8,128)(2,1)} %bitcast.20, f32[32,128]{1,0:T(8,128)} %bitcast.26, ...), custom_call_target="tpu_custom_call" | custom-call | tf_op jit(solution)/shard_map/pallas_call | solution.py:260
  28.0 24.2 %shard_map.87 = (f32[32,128]{1,0:T(8,128)}, bf16[2,16,128,128]{3,2,1,0:T(8,128)(2,1)}) custom-call(bf16[2,16,128,128]{3,2,1,0:T(8,128)(2,1)S(1)} %bitcast.19, f32[32,128]{1,0:T(8,128)S(1)} %get-tuple-element.11.mean_ref, bf16[2,8,32,4,128]{4,3,2,1,0:T(4,128)(2,1)S(1)} %get-tuple-element.12.z_ref, f32[8,8,128]{2,1,0:T(8,128)S(1)} %get-tuple-element.13.p_ref, ...), custom_call_target="tpu_custom_call" | custom-call | tf_op jit(solution)/shard_map/pallas_call | solution.py:459

commit v5 on v4

--- a/solution.py
+++ b/solution.py
@@ -14,7 +14,7 @@
 STEP_Y = 2
 LEAD = 2
 PER = 4
-SPLIT = (6, 6)
+SPLIT = (4, 6)
 
 
 def mm(a, b):
@@ -23,6 +23,14 @@
 
 def exact(a, b):
     return jnp.dot(a, b, precision=HI, preferred_element_type=F32)
+
+
+def mm3(a, b):
+    a1 = a.astype(BF)
+    a2 = (a - a1.astype(F32)).astype(BF)
+    b1 = b.astype(BF)
+    b2 = (b - b1.astype(F32)).astype(BF)
+    return mm(jnp.concatenate([a1, a2], axis=1), jnp.concatenate([b1, b1], axis=0)) + mm(a1, b2)
 
 
 def split3(x):
@@ -285,7 +293,7 @@
     )(*[pltpu.with_memory_space_constraint(a, pltpu.HBM) for a in (spread, mean, col, row, lev, var, val)])
 
 
-def chain(zx, zt, qx, dcol, ivcol, z_f32, ivar_row):
+def chain(zx, zt, dcol, z_f32, ivar_row):
     count, members = z_f32.shape
     dof = members - 1.0
     lane = lax.broadcasted_iota(jnp.int32, (count, members), 1)
@@ -311,10 +319,18 @@
     resid = eye - 2.0 * scale * gram + scale * scale * square
     inv = scale * (2.0 * eye - scale * gram)
     for _ in range(DOUBLINGS):
-        both = exact(jnp.concatenate([inv, resid], axis=0), resid)
+        both = mm3(jnp.concatenate([inv, resid], axis=0), resid)
         inv = inv + both[:members]
         resid = both[members:]
-    inv = inv + exact(inv, resid)
+    inv = inv + mm3(inv, resid)
+    return gram, vec, inv
+
+
+def chain_end(zx, qx, ivcol, gram, vec, inv):
+    members = gram.shape[0]
+    rhs = zx[...]
+    eye = jnp.where(lax.broadcasted_iota(jnp.int32, gram.shape, 0)
+                    == lax.broadcasted_iota(jnp.int32, gram.shape, 1), 1.0, 0.0).astype(F32)
 
     def more(state):
         step, miss, _ = state
@@ -359,25 +375,31 @@
 
     columns(gap(0), dcol)
     columns(1.0 / rows8(2, 0), ivcol)
-    chain(zx, zt.at[0], qx.at[0], dcol, ivcol, panel(0), wide(1.0 / rows8(2, 0)))
+    state = chain(zx, zt.at[0], dcol, panel(0), wide(1.0 / rows8(2, 0)))
+    chain_end(zx, qx.at[0], ivcol, *state)
     columns(gap(1), dcol)
     columns(1.0 / rows8(2, 1), ivcol)
     z1[...] = panel(1).astype(BF)
 
-    def cross(c, carry):
-        r = pl.ds(pl.multiple_of(c * 512, 512), 512)
-        z_c = z1[r, :]
+    def cross_fill(c):
         for i in range(count // 256):
             cut = slice(i * 256, (i + 1) * 256)
-            cov = mm(z_c, zt[0, :, cut])
-            gain[0, 0:512, cut] = (tap[pl.ds(4 * c, 4), :, cut].reshape(512, 256) * cov).astype(BF)
-        inc = mm(gain[0, 0:512, :], qx[0])
-        z1[r, :] = (z_c.astype(F32) - (0.5 * unit) * inc[:, :members]).astype(BF)
+            cov = mm(z1[c * 512:(c + 1) * 512, :], zt[0, :, cut])
+            gain[c % 2, 0:512, cut] = (tap[4 * c:4 * c + 4, :, cut].reshape(512, 256) * cov).astype(BF)
+
+    def cross_drain(c):
+        r = slice(c * 512, (c + 1) * 512)
+        inc = mm(gain[c % 2, 0:512, :], qx[0])
+        z1[r, :] = (z1[r, :].astype(F32) - (0.5 * unit) * inc[:, :members]).astype(BF)
         dcol[r, :] = dcol[r, :] - unit * inc[:, members:]
-        return carry
-
-    lax.fori_loop(0, count // 512, cross, 0)
-    chain(zx, zt.at[1], qx.at[1], dcol, ivcol, z1[...].astype(F32), wide(1.0 / rows8(2, 1)))
+
+    for c in range(count // 512 + 1):
+        if c > 0:
+            cross_drain(c - 1)
+        if c < count // 512:
+            cross_fill(c)
+    state = chain(zx, zt.at[1], dcol, z1[...].astype(F32), wide(1.0 / rows8(2, 1)))
+    chain_end(zx, qx.at[1], ivcol, *state)
 
     macc[...] = jnp.zeros_like(macc)
     lane = lax.broadcasted_iota(jnp.int32, (cols_x, members), 1)

time: 52.5 us -> 50.5 us (0.962)
  Pallas kernels: 51.6 us -> 49.8 us
    pallas_call x1, Pallas kernels: 24.2 us -> 23.1 us  [update(): pl.pallas_call(functools.partial(update_kernel, nx, ny, radius, step_y),...]
    pallas_call x1, Pallas kernels: 27.4 us -> 26.7 us  [gather(): pl.pallas_call(functools.partial(gather_kernel, nx, ny, radius, cols_x, r...]
where the time goes in v5:
time: 50.5 us; the launch traced here: 50.6 us
  Pallas kernels  49.8 us (99%)
  between operations  0.8 us (2%)
    pallas_call x1, Pallas kernels, gather(): pl.pallas_call(functools.partial(gather_kernel, nx, ny, radius, cols_x, r...  26.7 us
    pallas_call x1, Pallas kernels, update(): pl.pallas_call(functools.partial(update_kernel, nx, ny, radius, step_y),...  23.1 us

profile of v5, /device:TPU:1, one launch (start us, length us, event | category | flops | bytes accessed | tf_op | source)
XLA Modules:
  0.0 50.6 jit_solution(10672053692216657488)
XLA Ops:
  0.6 26.7 %shard_map.86 = (bf16[2,8,32,4,128]{4,3,2,1,0:T(4,128)(2,1)S(1)}, f32[8,8,128]{2,1,0:T(8,128)S(1)}, f32[4,16,128]{2,1,0:T(8,128)S(1)}, f32[24,128,1024]{2,1,0:T(...) custom-call(bf16[4096,128]{1,0:T(8,128)(2,1)} %bitcast.20, f32[32,128]{1,0:T(8,128)} %bitcast.26, ...), custom_call_target="tpu_custom_call" | custom-call | tf_op jit(solution)/shard_map/pallas_call | solution.py:268
  27.3 23.1 %shard_map.87 = (f32[32,128]{1,0:T(8,128)}, bf16[2,16,128,128]{3,2,1,0:T(8,128)(2,1)}) custom-call(bf16[2,16,128,128]{3,2,1,0:T(8,128)(2,1)S(1)} %bitcast.19, f32[32,128]{1,0:T(8,128)S(1)} %get-tuple-element.11.mean_ref, bf16[2,8,32,4,128]{4,3,2,1,0:T(4,128)(2,1)S(1)} %get-tuple-element.12.z_ref, f32[8,8,128]{2,1,0:T(8,128)S(1)} %get-tuple-element.13.p_ref, ...), custom_call_target="tpu_custom_call" | custom-call | tf_op jit(solution)/shard_map/pallas_call | solution.py:481

commit v6 on v5

--- a/solution.py
+++ b/solution.py
@@ -14,7 +14,7 @@
 STEP_Y = 2
 LEAD = 2
 PER = 4
-SPLIT = (4, 6)
+SPLIT = (2, 6)
 
 
 def mm(a, b):

time: 50.5 us -> 49.9 us (0.988)
  Pallas kernels: 49.8 us -> 49.2 us
    pallas_call x1, Pallas kernels: 26.7 us -> 26.1 us  [gather(): pl.pallas_call(functools.partial(gather_kernel, nx, ny, radius, cols_x, r...]
where the time goes in v6:
time: 49.9 us; the launch traced here: 50 us
  Pallas kernels  49.2 us (99%)
  between operations  0.8 us (2%)
    pallas_call x1, Pallas kernels, gather(): pl.pallas_call(functools.partial(gather_kernel, nx, ny, radius, cols_x, r...  26.1 us
    pallas_call x1, Pallas kernels, update(): pl.pallas_call(functools.partial(update_kernel, nx, ny, radius, step_y),...  23.1 us

profile of v6, /device:TPU:1, one launch (start us, length us, event | category | flops | bytes accessed | tf_op | source)
XLA Modules:
  0.0 50.0 jit_solution(14047667949852970499)
XLA Ops:
  0.6 26.1 %shard_map.86 = (bf16[2,8,32,4,128]{4,3,2,1,0:T(4,128)(2,1)S(1)}, f32[8,8,128]{2,1,0:T(8,128)S(1)}, f32[4,16,128]{2,1,0:T(8,128)S(1)}, f32[24,128,1024]{2,1,0:T(...) custom-call(bf16[4096,128]{1,0:T(8,128)(2,1)} %bitcast.20, f32[32,128]{1,0:T(8,128)} %bitcast.26, ...), custom_call_target="tpu_custom_call" | custom-call | tf_op jit(solution)/shard_map/pallas_call | solution.py:268
  26.7 23.1 %shard_map.87 = (f32[32,128]{1,0:T(8,128)}, bf16[2,16,128,128]{3,2,1,0:T(8,128)(2,1)}) custom-call(bf16[2,16,128,128]{3,2,1,0:T(8,128)(2,1)S(1)} %bitcast.19, f32[32,128]{1,0:T(8,128)S(1)} %get-tuple-element.11.mean_ref, bf16[2,8,32,4,128]{4,3,2,1,0:T(4,128)(2,1)S(1)} %get-tuple-element.12.z_ref, f32[8,8,128]{2,1,0:T(8,128)S(1)} %get-tuple-element.13.p_ref, ...), custom_call_target="tpu_custom_call" | custom-call | tf_op jit(solution)/shard_map/pallas_call | solution.py:481
